TPU v7x, 512 devices: a whole 4x8x8 slice. The times are simulated.
512 devices in a mesh: expert: 32 (over x, z), tensor: 8 (over y), dp: 2 (over core).
Axes of the slice: x: 4, y: 8, z: 8, core: 2. Of those that a mesh axis runs over, the one named last changes fastest.
Arguments:
- tokens: bfloat16 [4096, 7168], P(('expert', 'dp'), 'tensor'), may hold values from -6 to 6
- gate_weight: bfloat16 [32, 7168, 1024], P('expert', 'tensor', 'dp'), may hold values from -0.25 to 0.25
- up_weight: bfloat16 [32, 7168, 1024], P('expert', 'tensor', 'dp'), may hold values from -0.25 to 0.25
- down_weight: bfloat16 [32, 1024, 7168], P('expert', 'dp', 'tensor'), may hold values from -0.1875 to 0.1875
- sketch: bfloat16 [32, 2, 1024, 512], P('expert', None, 'dp'), may hold values from -6 to 6
- clusters: int32 [32], replicated, may hold values from 0 to 11, never falling along the last dimension, each value on 1 to 4 neighbouring positions
- routes: int32 [4096, 8], P(('expert', 'dp')), may hold values from 0 to 31, all different within a row; in each aligned block of 64 rows (0 to 63, 64 to 127, ...) at most 24 rows name the same one
- route_weights: float32 [4096, 8], P(('expert', 'dp')), may hold values from 0.05 to 0.3
Outputs:
- mixed: bfloat16 [4096, 7168], P(('expert', 'dp'), 'tensor')
Inputs may be any that keep to these rules, and one draw needn't show every extreme that they name: `clusters`: the experts of one cluster are consecutive; a cluster holds 1 to 4 experts, and one holds exactly 4. `routes`: A row names 8 different experts. In each aligned block of 64 rows (the rows of one device) no expert is named by more than 24 rows, a bound that some block reaches.
All inputs are finite; a program needn't handle non-finite values.
Results may differ from a plain program's by a relative error of at most 0.023.
Values may be sent and summed in bfloat16 or wider, within the bound.
A program may use at most 64 MiB of HBM per device.

v0:
```python
import jax
import jax.numpy as jnp
from jax import lax
from jax.sharding import PartitionSpec as P

MOST = 4


HIGHEST = lax.Precision.HIGHEST


def shifted(value, axis, steps):
    count = lax.axis_size(axis)
    initial, last = (max(0, -steps), min(count, count - steps))
    return lax.ppermute(value, axis, [(source, source + steps) for source in range(initial, last)])


def activate(projected, coefficients):
    gate_part = jnp.dot(projected, coefficients[0], preferred_element_type=jnp.float32)
    up_part = jnp.dot(projected, coefficients[1], preferred_element_type=jnp.float32)
    return (jax.nn.silu(gate_part) * up_part).astype(jnp.bfloat16)


def on_device(tokens, gate_weight, up_weight, down_weight, sketch, clusters, routes, route_weights):
    gate_rows = gate_weight[0]
    up_rows = up_weight[0]
    sketched = jnp.dot(gate_rows, sketch[0, 0], preferred_element_type=jnp.float32) + jnp.dot(
        up_rows, sketch[0, 1], preferred_element_type=jnp.float32
    )
    own_sketch = lax.psum_scatter(sketched, "dp", scatter_dimension=0, tiled=True)
    experts = lax.axis_size("expert")
    position = lax.axis_index("expert")
    my_cluster = clusters[position]
    summed = own_sketch
    for offset in range(1, MOST):
        below = shifted(own_sketch, "expert", offset)
        above = shifted(own_sketch, "expert", -offset)
        below_same = jnp.logical_and(
            position - offset >= 0, clusters[jnp.maximum(position - offset, 0)] == my_cluster
        )
        above_same = jnp.logical_and(
            position + offset < experts,
            clusters[jnp.minimum(position + offset, experts - 1)] == my_cluster,
        )
        summed = summed + jnp.where(below_same, below, 0.0) + jnp.where(above_same, above, 0.0)
    local_gram = lax.dot_general(summed, summed, (((0,), (0,)), ((), ())), precision=HIGHEST)
    gram = lax.psum(local_gram, ("tensor", "dp"))
    factor = jnp.linalg.cholesky(gram)
    basis_part = jax.scipy.linalg.solve_triangular(factor, summed.T, lower=True).T.astype(
        jnp.bfloat16
    )
    basis = lax.all_gather(basis_part, "dp", axis=0, tiled=True)
    gate_coeff = lax.dot_general(
        basis, gate_rows, (((0,), (0,)), ((), ())), preferred_element_type=jnp.float32
    )
    up_coeff = lax.dot_general(
        basis, up_rows, (((0,), (0,)), ((), ())), preferred_element_type=jnp.float32
    )
    partials = jnp.stack([gate_coeff, up_coeff]).astype(jnp.bfloat16)
    coeff_half = lax.psum(partials, "tensor").astype(jnp.float32).astype(jnp.bfloat16)
    coefficients, down_rows = (
        lax.all_gather(coeff_half, "dp", axis=2, tiled=True),
        lax.all_gather(down_weight[0], "dp", axis=0, tiled=True),
    )
    tok_rows = tokens.shape[0]
    top_count = routes.shape[1]
    capacity = tok_rows * top_count * 3 // (2 * experts)
    targets = routes.reshape(-1)
    assignments = targets.shape[0]
    onehot = (targets[:, None] == jnp.arange(experts, dtype=jnp.int32)[None, :]).astype(jnp.int32)
    place = jnp.sum((jnp.cumsum(onehot, axis=0) - 1) * onehot, axis=1)
    slot_index = targets * capacity + place
    owners = jnp.full((experts * capacity,), tok_rows, jnp.int32)
    owners = owners.at[slot_index].set(jnp.arange(assignments, dtype=jnp.int32) // top_count)
    padded = jnp.concatenate([tokens, jnp.zeros((1, tokens.shape[1]), tokens.dtype)], axis=0)
    outgoing = padded[owners].reshape(experts, capacity, tokens.shape[1])
    arrived = lax.all_to_all(outgoing, "expert", split_axis=0, concat_axis=0, tiled=True)
    arrived_rows = arrived.reshape(experts * capacity, tokens.shape[1])
    proj_part = jnp.dot(arrived_rows, basis, preferred_element_type=jnp.float32)
    projected = lax.psum(proj_part, "tensor").astype(jnp.bfloat16)
    hidden = activate(projected, coefficients)
    answers = jnp.dot(hidden, down_rows, preferred_element_type=jnp.float32).astype(jnp.bfloat16)
    returned = lax.all_to_all(
        answers.reshape(experts, capacity, tokens.shape[1]),
        "expert",
        split_axis=0,
        concat_axis=0,
        tiled=True,
    )
    picked = returned.reshape(experts * capacity, tokens.shape[1])[slot_index].astype(jnp.float32)
    weighted = picked * route_weights.reshape(-1)[:, None]
    return jnp.sum(weighted.reshape(tok_rows, top_count, tokens.shape[1]), axis=1).astype(
        jnp.bfloat16
    )


def solution(mesh):
    return jax.shard_map(
        on_device,
        mesh=mesh,
        in_specs=(
            P(("expert", "dp"), "tensor"),
            P("expert", "tensor", "dp"),
            P("expert", "tensor", "dp"),
            P("expert", "dp", "tensor"),
            P("expert", None, "dp", None),
            P(),
            P(("expert", "dp"), None),
            P(("expert", "dp"), None),
        ),
        out_specs=P(("expert", "dp"), "tensor"),
        check_vma=False,
    )
```

profile of v0, /device:TPU:6, one launch (start us, length us, event | category | flops | bytes accessed | tf_op | source)
XLA Modules:
  0.0 641.0 jit_solution(1484569244501889316)
XLA Ops:
  11.4 22.3 %reduce-scatter.2.cloned.1.call-done = f32[448,512]{1,0:T(8,128)} async-done(((f32[896,512]{1,0:T(8,128)}), f32[448,512]{1,0:T(8,128)}) %reduce-scatter.2.cloned.1.call-update) | async-done | bytes 917520 | tf_op jit(solution)/shard_map/reduce_scatter | solution.py:30
  37.3 4.5 collective-permute-start.1
  44.2 6.4 %collective-permute-start.3 = (f32[448,512]{1,0:T(8,128)}, f32[448,512]{1,0:T(8,128)}, u32[]{:S(2)}, u32[]{:S(2)}) collective-permute-start(f32[448,512]{1,0:T(8,128)} %reduce-scatter.2.cloned.1.call-done), channel_id=1, source_target_pairs={{32,0},{48,16},{64,32},{80,48},{96,64},{112,80},{128,96},{144,112}... | collective-permute-start | bytes 2752520 | tf_op jit(solution)/shard_map/ppermute | solution.py:15
  52.9 8.6 %collective-permute-done = f32[448,512]{1,0:T(8,128)S(1)} collective-permute-done((f32[448,512]{1,0:T(8,128)}, f32[448,512]{1,0:T(8,128)S(1)}, u32[]{:S(2)}, u32[]{:S(2)}) %collective-permute-start) | collective-permute-done | bytes 917536 | tf_op jit(solution)/shard_map/ppermute | solution.py:15
  61.5 5.1 collective-permute-start.5
  76.0 27.8 %collective-permute-done.2 = f32[448,512]{1,0:T(8,128)} collective-permute-done((f32[448,512]{1,0:T(8,128)}, f32[448,512]{1,0:T(8,128)}, u32[]{:S(2)}, u32[]{:S(2)}) %collective-permute-start.2) | collective-permute-done | bytes 917536 | tf_op jit(solution)/shard_map/ppermute | solution.py:15
  105.0 54.6 %collective-permute-done.4 = f32[448,512]{1,0:T(8,128)} collective-permute-done((f32[448,512]{1,0:T(8,128)}, f32[448,512]{1,0:T(8,128)}, u32[]{:S(2)}, u32[]{:S(2)}) %collective-permute-start.4) | collective-permute-done | bytes 917536 | tf_op jit(solution)/shard_map/ppermute | solution.py:15
  166.3 118.4 %all-reduce.6.cloned.1.call-done = f32[512,512]{0,1:T(8,128)} async-done(((f32[512,512]{0,1:T(8,128)}), f32[512,512]{0,1:T(8,128)}) %all-reduce.6.cloned.1.call-update) | async-done | bytes 1048592 | tf_op jit(solution)/shard_map/psum | solution.py:47
  289.8 11.7 %cholesky.104 = f32[128,128]{1,0:T(8,128)S(1)} custom-call(f32[128,128]{1,0:T(8,128)S(1)} %cholesky.266), custom_call_target="Cholesky" | custom-call | tf_op jit(solution)/shard_map/jit(cholesky)/cholesky | solution.py:48
  301.7 9.8 %custom-call.31 = f32[1,128,128]{1,2,0:T(8,128)S(1)} custom-call(f32[1,128,128]{2,1,0:T(8,128)S(1)} %get-tuple-element.32), custom_call_target="InvertDiagBlocksLowerTriangular" | custom-call | tf_op jit(solution)/shard_map/jit(cholesky)/cholesky | solution.py:48
  314.0 11.7 %cholesky.217 = f32[128,128]{1,0:T(8,128)S(1)} custom-call(f32[128,128]{1,0:T(8,128)S(1)} %cholesky.270), custom_call_target="Cholesky" | custom-call | tf_op jit(solution)/shard_map/jit(cholesky)/cholesky | solution.py:48
  325.8 10.0 %custom-call.32 = f32[1,128,128]{1,2,0:T(8,128)S(1)} custom-call(f32[1,128,128]{2,1,0:T(8,128)S(1)} %get-tuple-element.29), custom_call_target="InvertDiagBlocksLowerTriangular" | custom-call | tf_op jit(solution)/shard_map/jit(cholesky)/cholesky | solution.py:48
  337.3 11.7 %cholesky.238 = f32[128,128]{1,0:T(8,128)S(1)} custom-call(f32[128,128]{1,0:T(8,128)S(1)} %cholesky.275), custom_call_target="Cholesky" | custom-call | tf_op jit(solution)/shard_map/jit(cholesky)/cholesky | solution.py:48
  349.8 9.8 %custom-call.33 = f32[1,128,128]{1,2,0:T(8,128)S(1)} custom-call(f32[1,128,128]{2,1,0:T(8,128)S(1)} %get-tuple-element.26), custom_call_target="InvertDiagBlocksLowerTriangular" | custom-call | tf_op jit(solution)/shard_map/jit(cholesky)/cholesky | solution.py:48
  361.1 11.7 %cholesky.255 = f32[128,128]{1,0:T(8,128)S(1)} custom-call(f32[128,128]{1,0:T(8,128)S(1)} %convolution_subtract_fusion.2), custom_call_target="Cholesky" | custom-call | tf_op jit(solution)/shard_map/jit(cholesky)/cholesky | solution.py:48
  378.3 11.7 %while.1 = (s32[]{:T(128)}, f32[512,512]{1,0:T(8,128)}, s32[4,2]{0,1:T(2,128)S(1)}, f32[4,128,128]{2,1,0:T(8,128)S(1)}, s32[]{:T(128)}) while((s32[]{:T(128)}, f32[512,512]{1,0:T(8,128)}, s32[4,2]{0,1:T(2,128)S(1)}, f32[4,128,128]{2,1,0:T(8,128)S(1)}, s32[]{:T(128)}) %tuple.36), condition=%wide.while_cond, body=%wide.while_body.sunk | while | flops 2 | bytes 131181 | solution.py:49
  390.0 39.3 %custom-call.34 = f32[4,128,128]{1,2,0:T(8,128)S(1)} custom-call(f32[4,128,128]{2,1,0:T(8,128)S(1)} %get-tuple-element.12), custom_call_target="InvertDiagBlocksLowerTriangular" | custom-call | tf_op jit(solution)/shard_map/jit(_solve_triangular)/triangular_solve | solution.py:49
  446.9 10.5 %all-to-all-start = ((bf16[32,24,896]{2,1,0:T(8,128)(2,1)}), bf16[32,24,896]{2,1,0:T(8,128)(2,1)S(1)}, u32[]{:S(2)}, u32[]{:S(2)}) async-start(bf16[32,24,896]{2,1,0:T(8,128)(2,1)} %bitcast.3), calls=%async_computation | async-start | bytes 2752512 | tf_op jit(solution)/shard_map/all_to_all | solution.py:77
  457.5 65.5 %all-reduce.8.cloned.1.call-done = bf16[2,512,512]{2,1,0:T(8,128)(2,1)} async-done(((bf16[2,512,512]{2,1,0:T(8,128)(2,1)}), bf16[2,512,512]{2,1,0:T(8,128)(2,1)}) %all-reduce.8.cloned.1.call-update) | async-done | bytes 1048592 | tf_op jit(solution)/shard_map/psum | solution.py:60
  527.3 63.3 %all-reduce.9 = bf16[768,512]{1,0:T(8,128)(2,1)S(1)} all-reduce(f32[768,512]{1,0:T(8,128)S(1)} %fusion.68), channel_id=1, replica_groups=mesh['expert'=32,'tensor'=8,'dp'=2] {'tensor'}, use_global_device_ids=true, to_apply=%region_14.15 | all-reduce | flops 393216 | bytes 2359296 | tf_op jit(solution)/shard_map/psum | solution.py:80
  590.6 3.9 fusion.8
  594.5 6.5 %fusion.3 = bf16[768,896]{1,0:T(8,128)(2,1)} fusion(bf16[1,1024,896]{2,1,0:T(8,128)(2,1)} %all-gather.6.cloned.1.call-done, f32[768,1024]{1,0:T(8,128)} %fusion.8, bf16[2,512,1024]{2,1,0:T(8,128)(2,1)} %all-gather.4.cloned.1.call-done, bf16[768,512]{1,0:T(8,128)(2,1)S(1)} %all-reduce.9), kind=kOutput, calls=%fused_computation.10 | convolution fusion | flops 2219999232 | bytes 8192000 | tf_op jit(solution)/shard_map/dot_general | solution.py:82
  601.0 10.7 %all-to-all-start.1 = ((bf16[32,24,896]{2,1,0:T(8,128)(2,1)}), bf16[32,24,896]{2,1,0:T(8,128)(2,1)S(1)}, u32[]{:S(2)}, u32[]{:S(2)}) async-start(bf16[32,24,896]{2,1,0:T(8,128)(2,1)} %bitcast.130), calls=%async_computation.2 | async-start | bytes 2752512 | tf_op jit(solution)/shard_map/all_to_all | solution.py:83
  611.8 19.2 %all-to-all-done.1 = bf16[32,24,896]{2,1,0:T(8,128)(2,1)S(1)} async-done(((bf16[32,24,896]{2,1,0:T(8,128)(2,1)}), bf16[32,24,896]{2,1,0:T(8,128)(2,1)S(1)}, u32[]{:S(2)}, u32[]{:S(2)}) %all-to-all-start.1) | async-done | bytes 1376288 | tf_op jit(solution)/shard_map/all_to_all | solution.py:83
  (121 shorter events, 74.2 us)
Async XLA Ops:
  6.5 1.2 copy-start
  6.5 2.9 copy-start.4
  6.5 2.9 copy-start.5
  6.5 27.2 %reduce-scatter.2.cloned.1.call-start = ((), (), s32[]{:S(2)}) async-start(), calls=%async_computation.3 | async-start | bytes 2752512 | tf_op jit(solution)/shard_map/reduce_scatter | solution.py:30
  11.3 55.4 %copy-start.11 = (s32[64,8]{0,1:T(8,128)S(1)}, s32[64,8]{0,1:T(8,128)}, u32[]{:S(2)}) copy-start(s32[64,8]{0,1:T(8,128)} %param.14) | copy-start | bytes 6148
  11.3 55.6 %copy-start.10 = (s32[32]{0:T(128)S(1)}, s32[32]{0:T(128)}, u32[]{:S(2)}) copy-start(s32[32]{0:T(128)} %param.13) | copy-start | bytes 388
  11.3 273.3 %all-reduce.6.cloned.1.call-start = ((), (), s32[]{:S(2)}) async-start(), calls=%async_computation.4 | async-start | bytes 2097152 | tf_op jit(solution)/shard_map/psum | solution.py:47
  33.7 27.7 %collective-permute-start = (f32[448,512]{1,0:T(8,128)}, f32[448,512]{1,0:T(8,128)S(1)}, u32[]{:S(2)}, u32[]{:S(2)}) collective-permute-start(f32[448,512]{1,0:T(8,128)} %reduce-scatter.2.cloned.1.call-done), channel_id=1, source_target_pairs={{0,16},{16,32},{32,48},{48,64},{64,80},{80,96},{96,112},{112,128},... | collective-permute-start | bytes 2752520 | tf_op jit(solution)/shard_map/ppermute | solution.py:15
  37.3 38.7 %collective-permute-start.1 = (f32[448,512]{1,0:T(8,128)}, f32[448,512]{1,0:T(8,128)S(1)}, u32[]{:S(2)}, u32[]{:S(2)}) collective-permute-start(f32[448,512]{1,0:T(8,128)} %reduce-scatter.2.cloned.1.call-done), channel_id=1, source_target_pairs={{16,0},{32,16},{48,32},{64,48},{80,64},{96,80},{112,96},{128,112},... | collective-permute-start | bytes 2752520 | tf_op jit(solution)/shard_map/ppermute | solution.py:15
  41.8 62.0 %collective-permute-start.2 = (f32[448,512]{1,0:T(8,128)}, f32[448,512]{1,0:T(8,128)}, u32[]{:S(2)}, u32[]{:S(2)}) collective-permute-start(f32[448,512]{1,0:T(8,128)} %reduce-scatter.2.cloned.1.call-done), channel_id=1, source_target_pairs={{0,32},{16,48},{32,64},{48,80},{64,96},{80,112},{96,128},{112,144}... | collective-permute-start | bytes 2752520 | tf_op jit(solution)/shard_map/ppermute | solution.py:15
  44.2 60.8 %collective-permute-start.3 = (f32[448,512]{1,0:T(8,128)}, f32[448,512]{1,0:T(8,128)}, u32[]{:S(2)}, u32[]{:S(2)}) collective-permute-start(f32[448,512]{1,0:T(8,128)} %reduce-scatter.2.cloned.1.call-done), channel_id=1, source_target_pairs={{32,0},{48,16},{64,32},{80,48},{96,64},{112,80},{128,96},{144,112}... | collective-permute-start | bytes 2752520 | tf_op jit(solution)/shard_map/ppermute | solution.py:15
  50.7 109.0 %collective-permute-start.4 = (f32[448,512]{1,0:T(8,128)}, f32[448,512]{1,0:T(8,128)}, u32[]{:S(2)}, u32[]{:S(2)}) collective-permute-start(f32[448,512]{1,0:T(8,128)} %reduce-scatter.2.cloned.1.call-done), channel_id=1, source_target_pairs={{0,48},{16,64},{32,80},{48,96},{64,112},{80,128},{96,144},{112,160... | collective-permute-start | bytes 2752520 | tf_op jit(solution)/shard_map/ppermute | solution.py:15
  61.5 98.9 %collective-permute-start.5 = (f32[448,512]{1,0:T(8,128)}, f32[448,512]{1,0:T(8,128)}, u32[]{:S(2)}, u32[]{:S(2)}) collective-permute-start(f32[448,512]{1,0:T(8,128)} %reduce-scatter.2.cloned.1.call-done), channel_id=1, source_target_pairs={{48,0},{64,16},{80,32},{96,48},{112,64},{128,80},{144,96},{160,112... | collective-permute-start | bytes 2752520 | tf_op jit(solution)/shard_map/ppermute | solution.py:15
  76.0 83.7 %copy-start.8 = (f32[448,512]{1,0:T(8,128)}, f32[448,512]{1,0:T(8,128)S(1)}, u32[]{:S(2)}) copy-start(f32[448,512]{1,0:T(8,128)S(1)} %collective-permute-done.1) | copy-start | bytes 2752516
  165.5 357.5 %all-reduce.8.cloned.1.call-start = ((), (), s32[]{:S(2)}) async-start(), calls=%async_computation.5 | async-start | bytes 2097152 | tf_op jit(solution)/shard_map/psum | solution.py:60
  284.7 2.7 copy-start.1
  437.6 1.5 copy-start.6
  439.8 1.1 copy-start.9
  446.9 76.7 %all-to-all-start = ((bf16[32,24,896]{2,1,0:T(8,128)(2,1)}), bf16[32,24,896]{2,1,0:T(8,128)(2,1)S(1)}, u32[]{:S(2)}, u32[]{:S(2)}) async-start(bf16[32,24,896]{2,1,0:T(8,128)(2,1)} %bitcast.3), calls=%async_computation | async-start | bytes 2752512 | tf_op jit(solution)/shard_map/all_to_all | solution.py:77
  457.5 133.1 %all-gather.4.cloned.1.call-start = ((), (), s32[]{:S(2)}) async-start(), calls=%async_computation.6 | async-start | bytes 3145728 | tf_op jit(solution)/shard_map/all_gather | solution.py:62
  523.1 71.4 %all-gather.6.cloned.1.call-start = ((), (), s32[]{:S(2)}) async-start(), calls=%async_computation.7 | async-start | bytes 2752512 | tf_op jit(solution)/shard_map/all_gather | solution.py:63
  523.7 1.1 copy-start.3
  601.0 10.7 %copy-start.12 = (f32[64,8]{0,1:T(8,128)S(1)}, f32[64,8]{0,1:T(8,128)}, u32[]{:S(2)}) copy-start(f32[64,8]{0,1:T(8,128)} %param.15) | copy-start | bytes 6148
  601.0 30.0 %all-to-all-start.1 = ((bf16[32,24,896]{2,1,0:T(8,128)(2,1)}), bf16[32,24,896]{2,1,0:T(8,128)(2,1)S(1)}, u32[]{:S(2)}, u32[]{:S(2)}) async-start(bf16[32,24,896]{2,1,0:T(8,128)(2,1)} %bitcast.130), calls=%async_computation.2 | async-start | bytes 2752512 | tf_op jit(solution)/shard_map/all_to_all | solution.py:83
  (2 other events, 1.9 us)
Sparse Core Ops, SparseCore 0:
  11.5 22.2 reduce-scatter.1
  165.6 118.9 all-reduce.5
  441.0 81.9 all-reduce.7
  525.0 17.4 all-gather.3
  544.4 19.6 all-gather.5
where the time goes:
time: 649 us; the launch traced here: 641 us
  waiting for transfers between devices  319 us (49%)
  other arithmetic  127 us (20%)
  blocking collectives  65.7 us (10%)
  starting transfers between devices  45.8 us (7%)
  matrix products  32 us (5%)
  local copies, waits for them, and re-layouts  27.9 us (4%)
  between operations  23.6 us (4%)
    psum x1, waiting for transfers between devices, on_device(): gram = lax.psum(local_gram, ('tensor', 'dp'))  118 us
    ppermute x6, waiting for transfers between devices, shifted(): lax.ppermute(value, axis, [(source, source + steps) for source in range(i...  92.9 us
    another operation x14, other arithmetic, on_device(): factor = jnp.linalg.cholesky(gram)  79.1 us
    psum x1, waiting for transfers between devices, on_device(): lax.psum(partials, 'tensor').astype(jnp.float32).astype(jnp.bfloat16)  65.5 us
    psum x1, blocking collectives, on_device(): projected = lax.psum(proj_part, 'tensor').astype(jnp.bfloat16)  63.3 us
    another operation x3, other arithmetic, on_device(): jax.scipy.linalg.solve_triangular(factor, summed.T, lower=True)  40.4 us
    ppermute x6, starting transfers between devices, shifted(): lax.ppermute(value, axis, [(source, source + steps) for source in range(i...  24.3 us
    reduce_scatter x1, waiting for transfers between devices, on_device(): lax.psum_scatter(sketched, 'dp', scatter_dimension=0, tiled=True)  22.3 us
  transfers between devices with their start and end apart: 13, of which 9 were waited for; matrix products, arithmetic and copies ran while one was open for 2% of the time, Pallas kernels for 0%

commit v1 on v0

v1 whole, which is shorter than its diff:
```python
import jax
import jax.numpy as jnp
from jax import lax
from jax.experimental import pallas as pl
from jax.experimental.pallas import tpu as pltpu
from jax.sharding import PartitionSpec as P

HIGHEST = lax.Precision.HIGHEST
BLK = 128


def factor_block(tiles):
    lane = lax.broadcasted_iota(jnp.int32, (8, BLK), 1)
    sub = lax.broadcasted_iota(jnp.int32, (8, BLK), 0)
    n = BLK // 8
    tiles = list(tiles)
    for k in range(0, BLK, 2):
        t, r = divmod(k, 8)
        cur = tiles[t]
        col1 = jnp.broadcast_to(cur[:, k:k + 1], (8, BLK))
        col2 = jnp.broadcast_to(cur[:, k + 1:k + 2], (8, BLK))
        a = col1[r:r + 1, :]
        b = col1[r + 1:r + 2, :]
        c = col2[r + 1:r + 2, :]
        ra = 1.0 / a
        rc = a / (a * c - b * b)
        first, second = lane == k, lane == k + 1
        both = jnp.logical_or(first, second)
        row1 = jnp.where(first[:1], 1.0, jnp.where(second[:1], 0.0, cur[r:r + 1, :]))
        row2 = jnp.where(both[:1], 0.0, cur[r + 1:r + 2, :]) - (b * ra) * row1
        row2 = jnp.where(second[:1], 1.0, row2)
        v2 = rc * row2
        v1 = ra * row1 - (b * ra) * v2
        for i in range(t, n):
            old = tiles[i]
            if i == t:
                new = jnp.where(both, 0.0, old) - col1 * v1 - col2 * v2
                new = jnp.where(sub > r + 1, new, old)
                new = jnp.where(sub == r, row1 * jnp.sqrt(ra), new)
                new = jnp.where(sub == r + 1, row2 * jnp.sqrt(rc), new)
            else:
                c1 = jnp.broadcast_to(old[:, k:k + 1], (8, BLK))
                c2 = jnp.broadcast_to(old[:, k + 1:k + 2], (8, BLK))
                new = jnp.where(both, 0.0, old) - c1 * v1 - c2 * v2
            tiles[i] = new
    return [jnp.where(lane <= sub + 8 * i, tiles[i], 0.0) for i in range(n)]

def chol_kernel(g_ref, out_ref, inv_ref):
    size = g_ref.shape[0]
    steps = size // BLK
    out_ref[...] = g_ref[...]

    def step(j, carry):
        at = pl.multiple_of(j * BLK, BLK)
        tiles = [out_ref[pl.ds(pl.multiple_of(at + 8 * i, 8), 8), pl.ds(at, BLK)] for i in range(BLK // 8)]
        for i, tile in enumerate(factor_block(tiles)):
            inv_ref[8 * i:8 * i + 8, :] = tile
        inv = inv_ref[...]
        rows = lax.broadcasted_iota(jnp.int32, (BLK, BLK), 0)
        cols = lax.broadcasted_iota(jnp.int32, (BLK, BLK), 1)
        eye = jnp.where(rows == cols, 1.0, 0.0)
        out_ref[pl.ds(at, BLK), pl.ds(at, BLK)] = eye
        full = jnp.dot(inv, out_ref[pl.ds(at, BLK), :], precision=HIGHEST, preferred_element_type=jnp.float32)
        column = lax.broadcasted_iota(jnp.int32, (BLK, size), 1)
        later = jnp.where(column >= at + BLK, full, 0.0)
        out_ref[pl.ds(at, BLK), :] = full
        column = lax.broadcasted_iota(jnp.int32, (size, size), 1)
        row = lax.broadcasted_iota(jnp.int32, (size, size), 0)
        zero = (column >= at) & (column < at + BLK) & (row >= at + BLK)
        out_ref[...] = jnp.where(zero, 0.0, out_ref[...]) - lax.dot_general(
            later, full, (((0,), (0,)), ((), ())), precision=HIGHEST, preferred_element_type=jnp.float32)
        return carry

    lax.fori_loop(0, steps, step, 0)
    row = lax.broadcasted_iota(jnp.int32, (size, size), 0)
    column = lax.broadcasted_iota(jnp.int32, (size, size), 1)
    out_ref[...] = jnp.where(column <= row, out_ref[...], 0.0)

def inverse_factor(gram):
    size = gram.shape[0]
    return pl.pallas_call(
        chol_kernel,
        out_shape=jax.ShapeDtypeStruct((size, size), jnp.float32),
        in_specs=[pl.BlockSpec(memory_space=pltpu.VMEM)],
        out_specs=pl.BlockSpec(memory_space=pltpu.VMEM),
        scratch_shapes=[pltpu.VMEM((BLK, BLK), jnp.float32)],
        cost_estimate=pl.CostEstimate(flops=4 * size ** 3, bytes_accessed=8 * size * size, transcendentals=0),
    )(gram)

def split_dot(precise, plain, transposed):
    high = precise.astype(jnp.bfloat16)
    low = (precise - high.astype(jnp.float32)).astype(jnp.bfloat16)
    if transposed:
        dims = (((1,), (1,)), ((), ()))
        return lax.dot_general(plain, high, dims, preferred_element_type=jnp.float32) + lax.dot_general(
            plain, low, dims, preferred_element_type=jnp.float32)
    dims = (((1,), (0,)), ((), ()))
    return lax.dot_general(high, plain, dims, preferred_element_type=jnp.float32) + lax.dot_general(
        low, plain, dims, preferred_element_type=jnp.float32)


def sum_over(value, axis):
    count = lax.axis_size(axis)
    pieces = value.reshape((count, value.shape[0] // count) + value.shape[1:])
    arrived = lax.all_to_all(pieces, axis, split_axis=0, concat_axis=0, tiled=True)
    return jnp.sum(arrived.astype(jnp.float32), axis=0)


def transposed_dot(left, right):
    return lax.dot_general(left, right, (((0,), (0,)), ((), ())), preferred_element_type=jnp.float32)


def on_device(tokens, gate_weight, up_weight, down_weight, sketch, clusters, routes, route_weights):
    gate_rows = gate_weight[0]
    up_rows = up_weight[0]
    experts = lax.axis_size("expert")
    half = lax.axis_index("dp")
    sketched = jnp.dot(gate_rows, sketch[0, 0], preferred_element_type=jnp.float32) + jnp.dot(
        up_rows, sketch[0, 1], preferred_element_type=jnp.float32
    )
    rows, rank = sketched.shape
    part = rows // 2
    kept = lax.dynamic_slice_in_dim(sketched, half * part, part, 0)
    sent = lax.dynamic_slice_in_dim(sketched, (1 - half) * part, part, 0).astype(jnp.bfloat16)
    own = kept + lax.ppermute(sent, "dp", [(0, 1), (1, 0)]).astype(jnp.float32)
    across, down = experts // 4, rank // 4
    pieces = own.astype(jnp.bfloat16).reshape(across, part // across, 4, down).transpose(0, 2, 1, 3)
    pieces = pieces.reshape(experts, part // across, down)
    pieces = lax.all_to_all(pieces, "expert", split_axis=0, concat_axis=0, tiled=True)
    same = (clusters[:, None] == clusters[None, :]).astype(jnp.bfloat16)
    pieces = jnp.einsum("ef,frc->erc", same, pieces, preferred_element_type=jnp.float32).astype(jnp.bfloat16)
    pieces = lax.all_to_all(pieces, "expert", split_axis=0, concat_axis=0, tiled=True)
    summed = pieces.reshape(across, 4, part // across, down).transpose(0, 2, 1, 3).reshape(part, rank)
    summed = lax.all_gather(summed, "dp", axis=0, tiled=True)

    columns = lax.dynamic_slice_in_dim(summed, half * (rank // 2), rank // 2, 1)
    gram = sum_over(transposed_dot(summed, columns), "tensor")
    gram = lax.all_gather(gram, ("dp", "tensor"), axis=0, tiled=True)
    gram = jnp.concatenate([gram[:rank], gram[rank:]], axis=1)
    inverse = inverse_factor(gram)

    coeff = jnp.concatenate([transposed_dot(summed, gate_rows), transposed_dot(summed, up_rows)], axis=1)
    coeff = sum_over(coeff.astype(jnp.bfloat16), "tensor").astype(jnp.bfloat16)
    coeff = lax.all_gather(coeff, ("dp", "tensor"), axis=0, tiled=True)
    down_rows = lax.all_gather(down_weight[0], "dp", axis=0, tiled=False)

    tok_rows = tokens.shape[0]
    top_count = routes.shape[1]
    capacity = tok_rows * top_count * 3 // (2 * experts)
    targets = routes.reshape(-1)
    assignments = targets.shape[0]
    onehot = (targets[:, None] == jnp.arange(experts, dtype=jnp.int32)[None, :]).astype(jnp.int32)
    place = jnp.sum((jnp.cumsum(onehot, axis=0) - 1) * onehot, axis=1)
    slot_index = targets * capacity + place
    owners = jnp.full((experts * capacity,), tok_rows, jnp.int32)
    owners = owners.at[slot_index].set(jnp.arange(assignments, dtype=jnp.int32) // top_count)
    padded = jnp.concatenate([tokens, jnp.zeros((1, tokens.shape[1]), tokens.dtype)], axis=0)
    outgoing = padded[owners].reshape(experts, capacity, tokens.shape[1])
    arrived = lax.all_to_all(outgoing, "expert", split_axis=0, concat_axis=0, tiled=True)
    arrived_rows = arrived.reshape(experts * capacity, tokens.shape[1])

    raw = jnp.dot(arrived_rows, summed, preferred_element_type=jnp.float32).astype(jnp.bfloat16)
    raw = sum_over(raw, "tensor").astype(jnp.bfloat16)
    raw = lax.all_gather(raw, "tensor", axis=0, tiled=True)

    projected = split_dot(inverse, raw, True).astype(jnp.bfloat16)
    answers = 0.0
    for index in range(2):
        block = split_dot(inverse, coeff[index * rank:(index + 1) * rank], False).astype(jnp.bfloat16)
        hidden_half = block.shape[1] // 2
        gate_part = jnp.dot(projected, block[:, :hidden_half], preferred_element_type=jnp.float32)
        up_part = jnp.dot(projected, block[:, hidden_half:], preferred_element_type=jnp.float32)
        hidden = (jax.nn.silu(gate_part) * up_part).astype(jnp.bfloat16)
        answers = answers + jnp.dot(hidden, down_rows[index], preferred_element_type=jnp.float32)
    answers = answers.astype(jnp.bfloat16)
    returned = lax.all_to_all(
        answers.reshape(experts, capacity, tokens.shape[1]),
        "expert",
        split_axis=0,
        concat_axis=0,
        tiled=True,
    )
    picked = returned.reshape(experts * capacity, tokens.shape[1])[slot_index].astype(jnp.float32)
    weighted = picked * route_weights.reshape(-1)[:, None]
    return jnp.sum(weighted.reshape(tok_rows, top_count, tokens.shape[1]), axis=1).astype(
        jnp.bfloat16
    )


def solution(mesh):
    return jax.shard_map(
        on_device,
        mesh=mesh,
        in_specs=(
            P(("expert", "dp"), "tensor"),
            P("expert", "tensor", "dp"),
            P("expert", "tensor", "dp"),
            P("expert", "dp", "tensor"),
            P("expert", None, "dp", None),
            P(),
            P(("expert", "dp"), None),
            P(("expert", "dp"), None),
        ),
        out_specs=P(("expert", "dp"), "tensor"),
        check_vma=False,
    )
```

time: 649 us -> 331 us (0.51)
  waiting for transfers between devices: 319 us -> 132 us
  other arithmetic: 127 us -> 9.45 us
  Pallas kernels: 0 us -> 35 us
  local copies, waits for them, and re-layouts: 27.9 us -> 13.6 us
  between operations: 23.6 us -> 13.5 us
  blocking collectives: 65.7 us -> 56.2 us
    psum x2 -> x0, waiting for transfers between devices: 184 us -> none  [the longest x1 118 us: on_device(): gram = lax.psum(local_gram, ('tensor', 'dp'))]
    another operation x20 -> x2, other arithmetic: 122 us -> 1.2 us  [the longest x14 79.1 us: on_device(): factor = jnp.linalg.cholesky(gram)]
    ppermute x6 -> x1, waiting for transfers between devices: 92.9 us -> 1.91 us  [on_device(): own = kept + lax.ppermute(sent, 'dp', [(0, 1), (1, 0)]).astype(jnp.float32)]
    all_to_all x0 -> x4, waiting for transfers between devices: none -> 69.9 us  [the longest x3 56.2 us: sum_over(): lax.all_to_all(pieces, axis, split_axis=0, concat_axis=0, tiled=True)]
    psum x1 -> x0, blocking collectives: 63.3 us -> none  [on_device(): projected = lax.psum(proj_part, 'tensor').astype(jnp.bfloat16)]
    pallas_call x0 -> x1, Pallas kernels: none -> 35 us  [inverse_factor(): pl.pallas_call(chol_kernel, out_shape=jax.ShapeDtypeStruct((size, size),...]
    all_to_all x1, waiting for transfers between devices: 0.01 us -> 32.2 us  [on_device(): lax.all_to_all(outgoing, 'expert', split_axis=0, concat_axis=0, tiled=True)]
    all_to_all x0 -> x1, blocking collectives: none -> 27.7 us  [on_device(): lax.all_to_all(pieces, 'expert', split_axis=0, concat_axis=0, tiled=True)]
  transfers between devices with their start and end apart: 13 -> 10, of which waited for: 9 -> 7; matrix products, arithmetic and copies ran while one was open for 2% -> 9% of each run, Pallas kernels for 0% -> 11%
where the time goes in v1:
time: 331 us; the launch traced here: 328 us
  waiting for transfers between devices  132 us (40%)
  blocking collectives  56.2 us (17%)
  starting transfers between devices  40.4 us (12%)
  Pallas kernels  35 us (11%)
  matrix products  28 us (8%)
  local copies, waits for them, and re-layouts  13.6 us (4%)
  between operations  13.5 us (4%)
  other arithmetic  9.45 us (3%)
    all_to_all x3, waiting for transfers between devices, sum_over(): lax.all_to_all(pieces, axis, split_axis=0, concat_axis=0, tiled=True)  56.2 us
    pallas_call x1, Pallas kernels, inverse_factor(): pl.pallas_call(chol_kernel, out_shape=jax.ShapeDtypeStruct((size, size),...  35 us
    all_to_all x1, waiting for transfers between devices, on_device(): lax.all_to_all(outgoing, 'expert', split_axis=0, concat_axis=0, tiled=True)  32.2 us
    all_to_all x1, blocking collectives, on_device(): lax.all_to_all(pieces, 'expert', split_axis=0, concat_axis=0, tiled=True)  27.7 us
    all_to_all x1, waiting for transfers between devices, on_device(): lax.all_to_all(answers.reshape(experts, capacity, tokens.shape[1]), 'expe...  27 us
    all_gather x1, blocking collectives, on_device(): raw = lax.all_gather(raw, 'tensor', axis=0, tiled=True)  26 us
    all_to_all x3, starting transfers between devices, sum_over(): lax.all_to_all(pieces, axis, split_axis=0, concat_axis=0, tiled=True)  14.2 us
    all_to_all x1, waiting for transfers between devices, on_device(): lax.all_to_all(pieces, 'expert', split_axis=0, concat_axis=0, tiled=True)  13.7 us
  transfers between devices with their start and end apart: 10, of which 7 were waited for; matrix products, arithmetic and copies ran while one was open for 9% of the time, Pallas kernels for 11%

profile of v1, /device:TPU:6, one launch (start us, length us, event | category | flops | bytes accessed | tf_op | source)
XLA Modules:
  0.0 327.9 jit_solution(13758159584507215702)
XLA Ops:
  6.5 2.1 fusion.11
  14.6 27.7 %all_to_all.35 = bf16[32,56,128]{2,1,0:T(8,128)(2,1)S(1)} all-to-all(bf16[32,56,128]{2,1,0:T(8,128)(2,1)S(1)} %bitcast.85), channel_id=1, replica_groups=mesh['expert'=32,'tensor'=8,'dp'=2] {'expert'}, dimensions={0} | all-to-all | bytes 917504 | tf_op jit(solution)/shard_map/all_to_all | solution.py:129
  43.6 6.9 %all-to-all-start.2 = ((bf16[32,56,128]{2,1,0:T(8,128)(2,1)}), bf16[32,56,128]{2,1,0:T(8,128)(2,1)S(1)}, u32[]{:S(2)}, u32[]{:S(2)}) async-start(bf16[32,56,128]{2,1,0:T(8,128)(2,1)} %copy.25), calls=%async_computation.2 | async-start | bytes 917504 | tf_op jit(solution)/shard_map/all_to_all | solution.py:132
  50.5 13.7 %all-to-all-done.2 = bf16[32,56,128]{2,1,0:T(8,128)(2,1)S(1)} async-done(((bf16[32,56,128]{2,1,0:T(8,128)(2,1)}), bf16[32,56,128]{2,1,0:T(8,128)(2,1)S(1)}, u32[]{:S(2)}, u32[]{:S(2)}) %all-to-all-start.2) | async-done | bytes 458784 | tf_op jit(solution)/shard_map/all_to_all | solution.py:132
  64.4 2.5 all_gather.15
  68.2 7.1 %all-to-all-start.4 = ((f32[8,64,256]{2,1,0:T(8,128)}), f32[8,64,256]{2,1,0:T(8,128)S(1)}, u32[]{:S(2)}, u32[]{:S(2)}) async-start(f32[8,64,256]{2,1,0:T(8,128)} %bitcast.15), calls=%async_computation.4 | async-start | bytes 1048576 | tf_op jit(solution)/shard_map/all_to_all | solution.py:105
  78.9 14.2 %all-to-all-done.4 = f32[8,64,256]{2,1,0:T(8,128)S(1)} async-done(((f32[8,64,256]{2,1,0:T(8,128)}), f32[8,64,256]{2,1,0:T(8,128)S(1)}, u32[]{:S(2)}, u32[]{:S(2)}) %all-to-all-start.4) | async-done | bytes 524320 | tf_op jit(solution)/shard_map/all_to_all | solution.py:105
  93.1 3.6 %all-to-all-start.5 = ((bf16[8,64,1024]{2,1,0:T(8,128)(2,1)}), bf16[8,64,1024]{2,1,0:T(8,128)(2,1)S(1)}, u32[]{:S(2)}, u32[]{:S(2)}) async-start(bf16[8,64,1024]{2,1,0:T(8,128)(2,1)} %pad_maximum_fusion.1), calls=%async_computation.5 | async-start | bytes 2097152 | tf_op jit(solution)/shard_map/all_to_all | solution.py:105
  99.5 2.4 scatter_custom_fusion
  101.9 3.5 %gather_fusion = bf16[768,896]{1,0:T(8,128)(2,1)} fusion(bf16[65,896]{1,0:T(8,128)(2,1)S(1)} %concatenate.11, s32[1024]{0:T(1024)S(1)} %pad_clamp_fusion.1), kind=kCustom, calls=%fused_computation | custom fusion | bytes 2755584 | tf_op jit(solution)/shard_map/gather | solution.py:158
  105.4 22.2 %all-to-all-done.5 = bf16[8,64,1024]{2,1,0:T(8,128)(2,1)S(1)} async-done(((bf16[8,64,1024]{2,1,0:T(8,128)(2,1)}), bf16[8,64,1024]{2,1,0:T(8,128)(2,1)S(1)}, u32[]{:S(2)}, u32[]{:S(2)}) %all-to-all-start.5) | async-done | bytes 1048608 | tf_op jit(solution)/shard_map/all_to_all | solution.py:105
  127.7 7.1 %all-to-all-start = ((bf16[32,24,896]{2,1,0:T(8,128)(2,1)}), bf16[32,24,896]{2,1,0:T(8,128)(2,1)}, u32[]{:S(2)}, u32[]{:S(2)}) async-start(bf16[32,24,896]{2,1,0:T(8,128)(2,1)} %bitcast.3), calls=%async_computation | async-start | bytes 2752512 | tf_op jit(solution)/shard_map/all_to_all | solution.py:159
  135.7 32.2 %all-to-all-done = bf16[32,24,896]{2,1,0:T(8,128)(2,1)} async-done(((bf16[32,24,896]{2,1,0:T(8,128)(2,1)}), bf16[32,24,896]{2,1,0:T(8,128)(2,1)}, u32[]{:S(2)}, u32[]{:S(2)}) %all-to-all-start) | async-done | bytes 1376288 | tf_op jit(solution)/shard_map/all_to_all | solution.py:159
  168.0 3.2 convolution_convert_fusion
  171.2 3.5 %all-to-all-start.3 = ((bf16[8,96,512]{2,1,0:T(8,128)(2,1)}), bf16[8,96,512]{2,1,0:T(8,128)(2,1)S(1)}, u32[]{:S(2)}, u32[]{:S(2)}) async-start(bf16[8,96,512]{2,1,0:T(8,128)(2,1)} %bitcast.14), calls=%async_computation.3 | async-start | bytes 1572864 | tf_op jit(solution)/shard_map/all_to_all | solution.py:105
  175.5 19.8 %all-to-all-done.3 = bf16[8,96,512]{2,1,0:T(8,128)(2,1)S(1)} async-done(((bf16[8,96,512]{2,1,0:T(8,128)(2,1)}), bf16[8,96,512]{2,1,0:T(8,128)(2,1)S(1)}, u32[]{:S(2)}, u32[]{:S(2)}) %all-to-all-start.3) | async-done | bytes 786464 | tf_op jit(solution)/shard_map/all_to_all | solution.py:105
  195.4 26.0 %all_gather.16 = bf16[768,512]{1,0:T(8,128)(2,1)S(1)} all-gather(bf16[96,512]{1,0:T(8,128)(2,1)S(1)} %reduce_sum.55), channel_id=1, replica_groups=mesh['expert'=32,'tensor'=8,'dp'=2] {'tensor'}, dimensions={0}, use_global_device_ids=true | all-gather | bytes 884736 | tf_op jit(solution)/shard_map/all_gather | solution.py:164
  223.9 35.0 %shard_map.82 = f32[512,512]{1,0:T(8,128)} custom-call(f32[512,512]{1,0:T(8,128)} %pad_maximum_fusion.g_ref), custom_call_target="tpu_custom_call" | custom-call | flops 536870912 | bytes 2097152 | tf_op jit(solution)/shard_map/pallas_call | solution.py:81
  261.9 2.1 fusion.3
  270.8 4.9 %fusion.1 = f32[768,896]{1,0:T(8,128)} fusion(f32[768,512]{1,0:T(8,128)} %fusion.21, bf16[768,512]{1,0:T(8,128)(2,1)S(1)} %add_convert_fusion.3, bf16[2,512,896]{2,1,0:T(8,128)(2,1)} %all-gather.8.cloned.1.call-done, bf16[512,1024]{1,0:T(8,128)(2,1)} %copy-done.4), kind=kOutput, calls=%fused_computation.13 | convolution fusion | flops 1109655552 | bytes 6553600 | tf_op jit(solution)/shard_map/dot_general | solution.py:174
  275.7 5.1 %add_convert_fusion = bf16[768,896]{1,0:T(8,128)(2,1)} fusion(f32[768,896]{1,0:T(8,128)} %fusion.1, f32[768,512]{1,0:T(8,128)} %fusion.17, bf16[768,512]{1,0:T(8,128)(2,1)S(1)} %add_convert_fusion.3, bf16[2,512,896]{2,1,0:T(8,128)(2,1)} %all-gather.8.cloned.1.call-done, bf16[512,1024]{1,0:T(8,128)(2,1)S(1)} %copy-done.3), kind=kOutput, calls=%fused_computation.3 | convolution fusion | flops 1111031808 | bytes 7929856 | tf_op jit(solution)/shard_map/dot_general | solution.py:174
  280.8 10.1 %all-to-all-start.6 = ((bf16[32,24,896]{2,1,0:T(8,128)(2,1)}), bf16[32,24,896]{2,1,0:T(8,128)(2,1)S(1)}, u32[]{:S(2)}, u32[]{:S(2)}) async-start(bf16[32,24,896]{2,1,0:T(8,128)(2,1)} %bitcast.88), calls=%async_computation.6 | async-start | bytes 2752512 | tf_op jit(solution)/shard_map/all_to_all | solution.py:176
  291.1 27.0 %all-to-all-done.6 = bf16[32,24,896]{2,1,0:T(8,128)(2,1)S(1)} async-done(((bf16[32,24,896]{2,1,0:T(8,128)(2,1)}), bf16[32,24,896]{2,1,0:T(8,128)(2,1)S(1)}, u32[]{:S(2)}, u32[]{:S(2)}) %all-to-all-start.6) | async-done | bytes 1376288 | tf_op jit(solution)/shard_map/all_to_all | solution.py:176
  318.1 2.0 gather_fusion.1
  (80 shorter events, 30.3 us)
Async XLA Ops:
  6.5 2.1 copy-start
  6.5 2.1 copy-start.5
  9.4 3.8 %collective-permute-start = (bf16[448,512]{1,0:T(8,128)(2,1)S(1)}, bf16[448,512]{1,0:T(8,128)(2,1)}, u32[]{:S(2)}, u32[]{:S(2)}) collective-permute-start(bf16[448,512]{1,0:T(8,128)(2,1)S(1)} %dynamic-slice_convert_fusion), channel_id=1, source_target_pairs={{0,1},{1,0},{2,3},{3,2},{4,5},{5,4},{6,7},{7,6},{8,9},{9,8},{10,11... | collective-permute-start | bytes 1376264 | tf_op jit(solution)/shard_map/ppermute | solution.py:125
  14.4 27.9 %copy-start.10 = (s32[32]{0:T(128)S(1)}, s32[32]{0:T(128)}, u32[]{:S(2)}) copy-start(s32[32]{0:T(128)} %param.13) | copy-start | bytes 388
  43.6 20.6 %all-to-all-start.2 = ((bf16[32,56,128]{2,1,0:T(8,128)(2,1)}), bf16[32,56,128]{2,1,0:T(8,128)(2,1)S(1)}, u32[]{:S(2)}, u32[]{:S(2)}) async-start(bf16[32,56,128]{2,1,0:T(8,128)(2,1)} %copy.25), calls=%async_computation.2 | async-start | bytes 917504 | tf_op jit(solution)/shard_map/all_to_all | solution.py:132
  68.2 24.9 %all-to-all-start.4 = ((f32[8,64,256]{2,1,0:T(8,128)}), f32[8,64,256]{2,1,0:T(8,128)S(1)}, u32[]{:S(2)}, u32[]{:S(2)}) async-start(f32[8,64,256]{2,1,0:T(8,128)} %bitcast.15), calls=%async_computation.4 | async-start | bytes 1048576 | tf_op jit(solution)/shard_map/all_to_all | solution.py:105
  75.9 1.2 copy-start.6
  78.9 18.5 %copy-start.8 = (s32[64,8]{0,1:T(8,128)S(1)}, s32[64,8]{0,1:T(8,128)}, u32[]{:S(2)}) copy-start(s32[64,8]{0,1:T(8,128)} %param.14) | copy-start | bytes 6148
  78.9 20.4 %copy-start.7 = (bf16[64,896]{1,0:T(8,128)(2,1)S(1)}, bf16[64,896]{1,0:T(8,128)(2,1)}, u32[]{:S(2)}) copy-start(bf16[64,896]{1,0:T(8,128)(2,1)} %param.8) | copy-start | bytes 344068
  93.1 34.6 %all-to-all-start.5 = ((bf16[8,64,1024]{2,1,0:T(8,128)(2,1)}), bf16[8,64,1024]{2,1,0:T(8,128)(2,1)S(1)}, u32[]{:S(2)}, u32[]{:S(2)}) async-start(bf16[8,64,1024]{2,1,0:T(8,128)(2,1)} %pad_maximum_fusion.1), calls=%async_computation.5 | async-start | bytes 2097152 | tf_op jit(solution)/shard_map/all_to_all | solution.py:105
  96.6 124.8 %all-gather.4.cloned.1.call-start = ((), (), s32[]{:S(2)}) async-start(), calls=%async_computation.7 | async-start | bytes 1114112 | tf_op jit(solution)/shard_map/all_gather | solution.py:138
  127.7 40.3 %all-to-all-start = ((bf16[32,24,896]{2,1,0:T(8,128)(2,1)}), bf16[32,24,896]{2,1,0:T(8,128)(2,1)}, u32[]{:S(2)}, u32[]{:S(2)}) async-start(bf16[32,24,896]{2,1,0:T(8,128)(2,1)} %bitcast.3), calls=%async_computation | async-start | bytes 2752512 | tf_op jit(solution)/shard_map/all_to_all | solution.py:159
  134.8 127.1 %all-gather.6.cloned.1.call-start = ((), (), s32[]{:S(2)}) async-start(), calls=%async_computation.8 | async-start | bytes 2228224 | tf_op jit(solution)/shard_map/all_gather | solution.py:144
  171.2 24.1 %all-to-all-start.3 = ((bf16[8,96,512]{2,1,0:T(8,128)(2,1)}), bf16[8,96,512]{2,1,0:T(8,128)(2,1)S(1)}, u32[]{:S(2)}, u32[]{:S(2)}) async-start(bf16[8,96,512]{2,1,0:T(8,128)(2,1)} %bitcast.14), calls=%async_computation.3 | async-start | bytes 1572864 | tf_op jit(solution)/shard_map/all_to_all | solution.py:105
  174.7 96.1 %all-gather.8.cloned.1.call-start = ((), (), s32[]{:S(2)}) async-start(), calls=%async_computation.9 | async-start | bytes 2752512 | tf_op jit(solution)/shard_map/all_gather | solution.py:145
  261.9 2.1 copy-start.1
  264.8 2.5 copy-start.2
  268.1 1.0 copy-start.4
  270.8 4.9 %copy-start.3 = (bf16[512,1024]{1,0:T(8,128)(2,1)S(1)}, bf16[512,1024]{1,0:T(8,128)(2,1)}, u32[]{:S(2)}) copy-start(bf16[512,1024]{1,0:T(8,128)(2,1)} %copy-done.2) | copy-start | bytes 3145732
  280.8 10.1 %copy-start.9 = (f32[64,8]{0,1:T(8,128)S(1)}, f32[64,8]{0,1:T(8,128)}, u32[]{:S(2)}) copy-start(f32[64,8]{0,1:T(8,128)} %param.15) | copy-start | bytes 6148
  280.8 37.3 %all-to-all-start.6 = ((bf16[32,24,896]{2,1,0:T(8,128)(2,1)}), bf16[32,24,896]{2,1,0:T(8,128)(2,1)S(1)}, u32[]{:S(2)}, u32[]{:S(2)}) async-start(bf16[32,24,896]{2,1,0:T(8,128)(2,1)} %bitcast.88), calls=%async_computation.6 | async-start | bytes 2752512 | tf_op jit(solution)/shard_map/all_to_all | solution.py:176
Sparse Core Ops, SparseCore 0:
  99.6 41.8 all-gather.3
  143.6 42.1 all-gather.5
  188.0 19.4 all-gather.7

commit v2 on v1

v2 whole, which is shorter than its diff:
```python
import jax
import jax.numpy as jnp
from jax import lax
from jax.experimental import pallas as pl
from jax.experimental.pallas import tpu as pltpu
from jax.sharding import PartitionSpec as P

MESH = pl.DeviceIdType.MESH
HIGHEST = lax.Precision.HIGHEST
BLK = 128


def factor_block(tiles, serve):
    lane = lax.broadcasted_iota(jnp.int32, (8, BLK), 1)
    sub = lax.broadcasted_iota(jnp.int32, (8, BLK), 0)
    n = BLK // 8
    tiles = list(tiles)
    for k in range(0, BLK, 2):
        t, r = divmod(k, 8)
        cur = tiles[t]
        col1 = jnp.broadcast_to(cur[:, k:k + 1], (8, BLK))
        col2 = jnp.broadcast_to(cur[:, k + 1:k + 2], (8, BLK))
        a = col1[r:r + 1, :]
        b = col1[r + 1:r + 2, :]
        c = col2[r + 1:r + 2, :]
        ra = 1.0 / a
        rc = a / (a * c - b * b)
        first, second = lane == k, lane == k + 1
        both = jnp.logical_or(first, second)
        row1 = jnp.where(first[:1], 1.0, jnp.where(second[:1], 0.0, cur[r:r + 1, :]))
        row2 = jnp.where(both[:1], 0.0, cur[r + 1:r + 2, :]) - (b * ra) * row1
        row2 = jnp.where(second[:1], 1.0, row2)
        v2 = rc * row2
        v1 = ra * row1 - (b * ra) * v2
        for i in range(t, n):
            old = tiles[i]
            if i == t:
                new = jnp.where(both, 0.0, old) - col1 * v1 - col2 * v2
                new = jnp.where(sub > r + 1, new, old)
                new = jnp.where(sub == r, row1 * jnp.sqrt(ra), new)
                new = jnp.where(sub == r + 1, row2 * jnp.sqrt(rc), new)
            else:
                c1 = jnp.broadcast_to(old[:, k:k + 1], (8, BLK))
                c2 = jnp.broadcast_to(old[:, k + 1:k + 2], (8, BLK))
                new = jnp.where(both, 0.0, old) - c1 * v1 - c2 * v2
            tiles[i] = new
        if k % 32 == 30:
            serve(k // 32)
    return [jnp.where(lane <= sub + 8 * i, tiles[i], 0.0) for i in range(n)]

def eliminate(out_ref, inv_ref, serve):
    size = out_ref.shape[0]
    steps = size // BLK

    def step(j, carry):
        at = pl.multiple_of(j * BLK, BLK)
        tiles = [out_ref[pl.ds(pl.multiple_of(at + 8 * i, 8), 8), pl.ds(at, BLK)] for i in range(BLK // 8)]
        for i, tile in enumerate(factor_block(tiles, lambda turn: serve(4 * j + turn))):
            inv_ref[8 * i:8 * i + 8, :] = tile
        inv = inv_ref[...]
        rows = lax.broadcasted_iota(jnp.int32, (BLK, BLK), 0)
        cols = lax.broadcasted_iota(jnp.int32, (BLK, BLK), 1)
        eye = jnp.where(rows == cols, 1.0, 0.0)
        out_ref[pl.ds(at, BLK), pl.ds(at, BLK)] = eye
        full = jnp.dot(inv, out_ref[pl.ds(at, BLK), :], precision=HIGHEST, preferred_element_type=jnp.float32)
        column = lax.broadcasted_iota(jnp.int32, (BLK, size), 1)
        later = jnp.where(column >= at + BLK, full, 0.0)
        out_ref[pl.ds(at, BLK), :] = full
        column = lax.broadcasted_iota(jnp.int32, (size, size), 1)
        row = lax.broadcasted_iota(jnp.int32, (size, size), 0)
        zero = (column >= at) & (column < at + BLK) & (row >= at + BLK)
        out_ref[...] = jnp.where(zero, 0.0, out_ref[...]) - lax.dot_general(
            later, full, (((0,), (0,)), ((), ())), precision=HIGHEST, preferred_element_type=jnp.float32)
        return carry

    lax.fori_loop(0, steps, step, 0)
    row = lax.broadcasted_iota(jnp.int32, (size, size), 0)
    column = lax.broadcasted_iota(jnp.int32, (size, size), 1)
    out_ref[...] = jnp.where(column <= row, out_ref[...], 0.0)

REACH = 3
CUTS = 4


def cluster_kernel(part_ref, weight_ref, out_ref, stage, got, own, plus, minus, acc,
                   dp_send, dp_recv, up_send, up_recv, low_send, low_recv, fin_send, fin_recv):
    count = lax.axis_size("expert")
    me = lax.axis_index("expert")
    half = lax.axis_index("dp")
    sibling = {"dp": 1 - half}
    after = {"expert": lax.rem(me + 1, count)}
    before = {"expert": lax.rem(me + count - 1, count)}
    part = part_ref.shape[0] // 2
    size = part // CUTS
    barrier = pltpu.get_barrier_semaphore()
    for device in (sibling, after, before):
        pl.semaphore_signal(barrier, inc=1, device_id=device, device_id_type=MESH)

    def rows(side, cut):
        return pl.ds(pl.multiple_of(side * part + cut * size, 16), size)

    def remote(src, dst, send, recv, device):
        return pltpu.make_async_remote_copy(
            src_ref=src, dst_ref=dst, send_sem=send, recv_sem=recv, device_id=device, device_id_type=MESH)

    def swap(cut):
        return remote(stage.at[cut], got.at[cut], dp_send.at[cut], dp_recv.at[cut], sibling)

    def ahead(hop, cut):
        source = own.at[cut] if hop == 0 else plus.at[hop - 1, cut]
        return remote(source, plus.at[hop, cut], up_send.at[hop, cut], up_recv.at[hop, cut], after)

    def back(hop, cut):
        source = own.at[cut] if hop == 0 else minus.at[hop - 1, cut]
        return remote(source, minus.at[hop, cut], low_send.at[hop, cut], low_recv.at[hop, cut], before)

    def finish(cut):
        place = out_ref.at[rows(half, cut)]
        return remote(place, place, fin_send.at[cut], fin_recv.at[cut], sibling)

    for cut in range(CUTS):
        stage[cut] = part_ref[rows(1 - half, cut), :].astype(jnp.bfloat16)
    pl.semaphore_wait(barrier, 3)
    for cut in range(CUTS):
        swap(cut).start()
    for cut in range(CUTS):
        swap(cut).wait_recv()
        value = (part_ref[rows(half, cut), :] + got[cut].astype(jnp.float32)).astype(jnp.bfloat16)
        own[cut] = value
        ahead(0, cut).start()
        back(0, cut).start()
        acc[cut] = value.astype(jnp.float32)
    for hop in range(REACH):
        for cut in range(CUTS):
            ahead(hop, cut).wait_recv()
            if hop < REACH - 1:
                ahead(hop + 1, cut).start()
            back(hop, cut).wait_recv()
            if hop < REACH - 1:
                back(hop + 1, cut).start()
            total = acc[cut] + weight_ref[hop:hop + 1, :] * plus[hop, cut].astype(jnp.float32)
            total = total + weight_ref[REACH + hop:REACH + hop + 1, :] * minus[hop, cut].astype(jnp.float32)
            if hop < REACH - 1:
                acc[cut] = total
            else:
                out_ref[rows(half, cut), :] = total.astype(jnp.bfloat16)
                finish(cut).start()
    for cut in range(CUTS):
        finish(cut).wait_recv()
        finish(cut).wait_send()
        swap(cut).wait_send()
        for hop in range(REACH):
            ahead(hop, cut).wait_send()
            back(hop, cut).wait_send()


def cluster_sum(sketched, weights):
    rows, rank = sketched.shape
    size = rows // 2 // CUTS
    return pl.pallas_call(
        cluster_kernel,
        out_shape=jax.ShapeDtypeStruct((rows, rank), jnp.bfloat16),
        in_specs=[pl.BlockSpec(memory_space=pltpu.VMEM)] * 2,
        out_specs=pl.BlockSpec(memory_space=pltpu.VMEM),
        scratch_shapes=[
            pltpu.VMEM((CUTS, size, rank), jnp.bfloat16),
            pltpu.VMEM((CUTS, size, rank), jnp.bfloat16),
            pltpu.VMEM((CUTS, size, rank), jnp.bfloat16),
            pltpu.VMEM((REACH, CUTS, size, rank), jnp.bfloat16),
            pltpu.VMEM((REACH, CUTS, size, rank), jnp.bfloat16),
            pltpu.VMEM((CUTS, size, rank), jnp.float32),
            pltpu.SemaphoreType.DMA((CUTS,)),
            pltpu.SemaphoreType.DMA((CUTS,)),
            pltpu.SemaphoreType.DMA((REACH, CUTS)),
            pltpu.SemaphoreType.DMA((REACH, CUTS)),
            pltpu.SemaphoreType.DMA((REACH, CUTS)),
            pltpu.SemaphoreType.DMA((REACH, CUTS)),
            pltpu.SemaphoreType.DMA((CUTS,)),
            pltpu.SemaphoreType.DMA((CUTS,)),
        ],
        compiler_params=pltpu.CompilerParams(collective_id=3, has_side_effects=True),
        cost_estimate=pl.CostEstimate(flops=10 ** 10, bytes_accessed=8 * rows * rank, transcendentals=0),
    )(sketched, weights)


def gram_kernel(part_ref, down_ref, out_ref, other_ref, arrive, pieces, rs_send, rs_recv, ag_send, ag_recv, sib_send, sib_recv, down_send, down_recv):
    me = lax.axis_index("tensor")
    half = lax.axis_index("dp")
    count = part_ref.shape[0]
    height, width = part_ref.shape[1:]
    sibling = {"dp": 1 - half}
    barrier = pltpu.get_barrier_semaphore()
    for step in range(1, count):
        pl.semaphore_signal(barrier, inc=1, device_id={"tensor": lax.rem(me + step, count)}, device_id_type=MESH)
    pl.semaphore_signal(barrier, inc=1, device_id=sibling, device_id_type=MESH)
    pl.semaphore_wait(barrier, count)

    def scatter(step):
        peer = lax.rem(me + step, count)
        return pltpu.make_async_remote_copy(
            src_ref=part_ref.at[peer], dst_ref=arrive.at[step], send_sem=rs_send.at[step], recv_sem=rs_recv.at[step],
            device_id={"tensor": peer}, device_id_type=MESH)

    def spread(step):
        peer = lax.rem(me + step, count)
        mine = half * count + me
        return pltpu.make_async_remote_copy(
            src_ref=pieces.at[mine], dst_ref=pieces.at[mine], send_sem=ag_send.at[step], recv_sem=ag_recv.at[step],
            device_id={"tensor": peer}, device_id_type=MESH)

    def hand(step):
        piece = half * count + lax.rem(me + count - step, count)
        return pltpu.make_async_remote_copy(
            src_ref=pieces.at[piece], dst_ref=pieces.at[piece], send_sem=sib_send.at[step], recv_sem=sib_recv.at[step],
            device_id=sibling, device_id_type=MESH)

    down = pltpu.make_async_remote_copy(
        src_ref=down_ref, dst_ref=other_ref, send_sem=down_send, recv_sem=down_recv,
        device_id=sibling, device_id_type=MESH)
    order = [4, 3, 5, 2, 6, 1, 7]
    for step in order:
        scatter(step).start()
    down.start()
    total = part_ref[me]
    for step in reversed(order):
        scatter(step).wait_recv()
        total = total + arrive[step]
    pieces[half * count + me] = total
    for step in order:
        spread(step).start()
    hand(0).start()
    for step in reversed(order):
        spread(step).wait_recv()
        hand(step).start()
    for step in range(count):
        hand(step).wait_recv()
    for side in range(2):
        for piece in range(count):
            out_ref[piece * height:(piece + 1) * height, side * width:(side + 1) * width] = pieces[side * count + piece]
    for step in order:
        scatter(step).wait_send()
        spread(step).wait_send()
    for step in range(count):
        hand(step).wait_send()
    down.wait()


def gram_sum(part, down):
    count, height, width = part.shape
    size = count * height
    return pl.pallas_call(
        gram_kernel,
        out_shape=[jax.ShapeDtypeStruct((size, size), jnp.float32), jax.ShapeDtypeStruct(down.shape, down.dtype)],
        in_specs=[pl.BlockSpec(memory_space=pltpu.VMEM), pl.BlockSpec(memory_space=pl.ANY)],
        out_specs=[pl.BlockSpec(memory_space=pltpu.VMEM), pl.BlockSpec(memory_space=pl.ANY)],
        scratch_shapes=[
            pltpu.VMEM((count, height, width), jnp.float32),
            pltpu.VMEM((2 * count, height, width), jnp.float32),
        ] + [pltpu.SemaphoreType.DMA((count,))] * 6 + [pltpu.SemaphoreType.DMA] * 2,
        compiler_params=pltpu.CompilerParams(collective_id=1, has_side_effects=True),
        cost_estimate=pl.CostEstimate(flops=40 * 10 ** 9, bytes_accessed=8 * size * size, transcendentals=0),
    )(part, down)


def factor_kernel(gram_ref, coeff_ref, raw_ref, out_ref, coeff_all, raw_all, inv_ref, coeff_slot, raw_slot,
                  send, recv, sib_send, sib_recv):
    count = coeff_ref.shape[1]
    hops = count - 1
    me = lax.axis_index("tensor")
    half = lax.axis_index("dp")
    sibling = {"dp": 1 - half}
    neighbours = ({"tensor": lax.rem(me + 1, count)}, {"tensor": lax.rem(me + hops, count)})
    barrier = pltpu.get_barrier_semaphore()
    for device in (sibling,) + neighbours:
        pl.semaphore_signal(barrier, inc=1, device_id=device, device_id_type=MESH)
    pl.semaphore_wait(barrier, 3)

    def chunk(side, distance):
        return lax.rem(me + (2 * count - distance if side == 0 else distance), count)

    def place(kind, side, index):
        return coeff_all.at[0, side, index] if kind == 0 else raw_all.at[side, index]

    def remote(src, dst, kind, side, turn):
        return pltpu.make_async_remote_copy(
            src_ref=src, dst_ref=dst, send_sem=send.at[kind, side, turn], recv_sem=recv.at[kind, side, turn],
            device_id=neighbours[side], device_id_type=MESH)

    def first(kind, side):
        part = (coeff_ref, raw_ref)[kind].at[side, chunk(side, 1)]
        return remote(part, (coeff_slot, raw_slot)[kind].at[side, 0], kind, side, 0)

    def add_on(kind, side, turn):
        slot = (coeff_slot, raw_slot)[kind]
        return remote(slot.at[side, turn - 1], slot.at[side, turn], kind, side, turn)

    def pass_on(kind, side, turn):
        here = place(kind, side, chunk(side, turn - hops))
        return remote(here, here, kind, side, turn)

    def share(side, number):
        index = chunk(side, number)
        return pltpu.make_async_remote_copy(
            src_ref=coeff_all.at[0, side, index], dst_ref=coeff_all.at[1, side, index],
            send_sem=sib_send.at[side, number], recv_sem=sib_recv.at[side, number],
            device_id=sibling, device_id_type=MESH)

    both = [(kind, side) for kind in range(2) for side in range(2)]
    for kind, side in both:
        first(kind, side).start()

    def serve(turn):
        @pl.when(turn < hops)
        def _():
            for kind, side in both:
                slot = (coeff_slot, raw_slot)[kind]
                remote(slot.at[side, turn], slot.at[side, turn], kind, side, turn).wait_recv()
                part = (coeff_ref, raw_ref)[kind][side, chunk(side, turn + 2)]
                value = (slot[side, turn].astype(jnp.float32) + part.astype(jnp.float32)).astype(jnp.bfloat16)

                @pl.when(turn < hops - 1)
                def _():
                    slot[side, turn] = value
                    add_on(kind, side, turn + 1).start()

                @pl.when(turn == hops - 1)
                def _():
                    place(kind, side, me)[...] = value
                    pass_on(kind, side, turn + 1).start()
                    if kind == 0:
                        share(side, 0).start()

        @pl.when((turn >= hops) & (turn < 2 * hops))
        def _():
            for kind, side in both:
                here = place(kind, side, chunk(side, turn - hops + 1))
                remote(here, here, kind, side, turn).wait_recv()

                @pl.when(turn < 2 * hops - 1)
                def _():
                    pass_on(kind, side, turn + 1).start()

                if kind == 0:
                    share(side, turn - hops + 1).start()

    out_ref[...] = gram_ref[...]
    eliminate(out_ref, inv_ref, serve)

    for kind, side in both:
        first(kind, side).wait_send()

    def drain(turn, carry):
        for kind, side in both:
            @pl.when(turn < hops)
            def _():
                add_on(kind, side, turn).wait_send()

            @pl.when(turn >= hops)
            def _():
                pass_on(kind, side, turn).wait_send()
        return carry

    lax.fori_loop(1, 2 * hops, drain, 0)

    def shared(number, carry):
        for side in range(2):
            share(side, number).wait_send()
            share(side, number).wait_recv()
        return carry

    lax.fori_loop(0, count, shared, 0)


def inverse_and_sums(gram, coeff, raw):
    size = gram.shape[0]
    count = coeff.shape[1]
    steps = 2 * (count - 1)
    slots = lambda array: (2, count - 1) + array.shape[2:]
    return pl.pallas_call(
        factor_kernel,
        out_shape=[
            jax.ShapeDtypeStruct((size, size), jnp.float32),
            jax.ShapeDtypeStruct((2,) + coeff.shape, jnp.bfloat16),
            jax.ShapeDtypeStruct(raw.shape, jnp.bfloat16),
        ],
        in_specs=[pl.BlockSpec(memory_space=pltpu.VMEM)] * 3,
        out_specs=[pl.BlockSpec(memory_space=pltpu.VMEM)] * 3,
        scratch_shapes=[
            pltpu.VMEM((BLK, BLK), jnp.float32),
            pltpu.VMEM(slots(coeff), jnp.bfloat16),
            pltpu.VMEM(slots(raw), jnp.bfloat16),
            pltpu.SemaphoreType.DMA((2, 2, steps)),
            pltpu.SemaphoreType.DMA((2, 2, steps)),
            pltpu.SemaphoreType.DMA((2, count)),
            pltpu.SemaphoreType.DMA((2, count)),
        ],
        compiler_params=pltpu.CompilerParams(collective_id=2, has_side_effects=True),
        cost_estimate=pl.CostEstimate(flops=40 * 10 ** 9, bytes_accessed=8 * size * size, transcendentals=0),
    )(gram, coeff, raw)


def split_dot(precise, plain, transposed):
    high = precise.astype(jnp.bfloat16)
    low = (precise - high.astype(jnp.float32)).astype(jnp.bfloat16)
    if transposed:
        dims = (((1,), (1,)), ((), ()))
        return lax.dot_general(plain, high, dims, preferred_element_type=jnp.float32) + lax.dot_general(
            plain, low, dims, preferred_element_type=jnp.float32)
    dims = (((1,), (0,)), ((), ()))
    return lax.dot_general(high, plain, dims, preferred_element_type=jnp.float32) + lax.dot_general(
        low, plain, dims, preferred_element_type=jnp.float32)


def transposed_dot(left, right):
    return lax.dot_general(left, right, (((0,), (0,)), ((), ())), preferred_element_type=jnp.float32)


def on_device(tokens, gate_weight, up_weight, down_weight, sketch, clusters, routes, route_weights):
    gate_rows = gate_weight[0]
    up_rows = up_weight[0]
    experts = lax.axis_size("expert")
    tensors = lax.axis_size("tensor")
    half = lax.axis_index("dp")
    position = lax.axis_index("expert")
    sketched = jnp.dot(gate_rows, sketch[0, 0], preferred_element_type=jnp.float32) + jnp.dot(
        up_rows, sketch[0, 1], preferred_element_type=jnp.float32
    )
    rank = sketched.shape[1]

    offsets = jnp.array([-1, -2, -3, 1, 2, 3, 0, 0], jnp.int32)
    others = position + offsets
    inside = (others >= 0) & (others < experts)
    same = inside & (clusters[jnp.clip(others, 0, experts - 1)] == clusters[position])
    weights = jnp.broadcast_to(same.astype(jnp.float32)[:, None], (8, rank))
    summed = cluster_sum(sketched, weights)

    tok_rows, width = tokens.shape
    top_count = routes.shape[1]
    capacity = tok_rows * top_count * 3 // (2 * experts)
    named = routes.T[None] == jnp.arange(experts, dtype=jnp.int32)[:, None, None]
    chosen = jnp.any(named, axis=1)
    shares = jnp.sum(jnp.where(named, route_weights.T[None], 0.0), axis=1)
    token_index = jnp.arange(tok_rows)
    earlier = (token_index[:, None] < token_index[None, :]).astype(jnp.bfloat16)
    place = jnp.dot(chosen.astype(jnp.bfloat16), earlier, preferred_element_type=jnp.float32).astype(jnp.int32)
    holds = chosen[:, None, :] & (place[:, None, :] == jnp.arange(capacity, dtype=jnp.int32)[None, :, None])
    select = holds.astype(jnp.bfloat16).reshape(experts * capacity, tok_rows)
    outgoing = jnp.dot(select, tokens, preferred_element_type=jnp.float32).astype(jnp.bfloat16)
    outgoing = outgoing.reshape(experts, capacity, width)

    columns = lax.dynamic_slice_in_dim(summed, half * (rank // 2), rank // 2, 1)
    gram = transposed_dot(summed, columns).reshape(tensors, rank // tensors, rank // 2)
    coeff = jnp.stack([transposed_dot(summed, gate_rows), transposed_dot(summed, up_rows)]).astype(jnp.bfloat16)
    coeff = coeff.reshape(2, tensors, rank // tensors, coeff.shape[2])
    gram, outgoing, coeff = lax.optimization_barrier((gram, outgoing, coeff))
    arrived = lax.all_to_all(outgoing, "expert", split_axis=0, concat_axis=0, tiled=True)
    gram, down_other = gram_sum(gram, down_weight[0])
    arrived, gram = lax.optimization_barrier((arrived, gram))
    raw = jnp.dot(arrived.reshape(experts * capacity, width), summed, preferred_element_type=jnp.float32)
    raw = raw.astype(jnp.bfloat16).reshape(2, tensors, experts * capacity // (2 * tensors), rank)
    inverse, coeff, raw = inverse_and_sums(gram, coeff, raw)

    projected = split_dot(inverse, raw.reshape(experts * capacity, rank), True).astype(jnp.bfloat16)
    answers = 0.0
    for index, down_rows in enumerate((down_weight[0], down_other)):
        gate_coeff = split_dot(inverse, coeff[index, 0].reshape(rank, -1), False).astype(jnp.bfloat16)
        up_coeff = split_dot(inverse, coeff[index, 1].reshape(rank, -1), False).astype(jnp.bfloat16)
        gate_part = jnp.dot(projected, gate_coeff, preferred_element_type=jnp.float32)
        up_part = jnp.dot(projected, up_coeff, preferred_element_type=jnp.float32)
        hidden = (jax.nn.silu(gate_part) * up_part).astype(jnp.bfloat16)
        answers = answers + jnp.dot(hidden, down_rows, preferred_element_type=jnp.float32)
    answers = answers.astype(jnp.bfloat16).reshape(experts, capacity, width)
    returned = lax.all_to_all(answers, "expert", split_axis=0, concat_axis=0, tiled=True)
    returned = returned.reshape(experts * capacity, width)
    mixing = jnp.where(holds, shares[:, None, :], 0.0).reshape(experts * capacity, tok_rows)
    high = mixing.astype(jnp.bfloat16)
    low = (mixing - high.astype(jnp.float32)).astype(jnp.bfloat16)
    return (transposed_dot(high, returned) + transposed_dot(low, returned)).astype(jnp.bfloat16)


def solution(mesh):
    return jax.shard_map(
        on_device,
        mesh=mesh,
        in_specs=(
            P(("expert", "dp"), "tensor"),
            P("expert", "tensor", "dp"),
            P("expert", "tensor", "dp"),
            P("expert", "dp", "tensor"),
            P("expert", None, "dp", None),
            P(),
            P(("expert", "dp"), None),
            P(("expert", "dp"), None),
        ),
        out_specs=P(("expert", "dp"), "tensor"),
        check_vma=False,
    )
```

time: 331 us -> 250 us (0.76)
  Pallas kernels: 35 us -> 149 us
  waiting for transfers between devices: 132 us -> 29 us
  blocking collectives: 56.2 us -> 0 us
  starting transfers between devices: 40.4 us -> 18.5 us
  between operations: 13.5 us -> 0.21 us
  matrix products: 28 us -> 39.8 us
  local copies, waits for them, and re-layouts: 13.6 us -> 6.37 us
  other arithmetic: 9.45 us -> 5.4 us
    pallas_call x1 -> x3, Pallas kernels: 35 us -> 149 us  [the longest x1 66.7 us: inverse_and_sums(): pl.pallas_call(factor_kernel, out_shape=[jax.ShapeDtypeStruct((size, size...]
    all_to_all x5 -> x1, waiting for transfers between devices: 96.9 us -> 29 us  [on_device(): lax.all_to_all(answers, 'expert', split_axis=0, concat_axis=0, tiled=True)]
    all_to_all x1, waiting for transfers between devices: 32.2 us -> 0.01 us  [on_device(): lax.all_to_all(outgoing, 'expert', split_axis=0, concat_axis=0, tiled=True)]
    all_gather x2 -> x0, blocking collectives: 28.5 us -> none  [the longest x1 26 us: on_device(): raw = lax.all_gather(raw, 'tensor', axis=0, tiled=True)]
    all_to_all x1 -> x0, blocking collectives: 27.7 us -> none  [on_device(): lax.all_to_all(pieces, 'expert', split_axis=0, concat_axis=0, tiled=True)]
    all_to_all x5 -> x1, starting transfers between devices: 31.2 us -> 10.3 us  [on_device(): lax.all_to_all(answers, 'expert', split_axis=0, concat_axis=0, tiled=True)]
    dot_general x6 -> x8, matrix products: 17 us -> 22.9 us  [the longest x2 9.01 us: on_device(): jnp.dot(hidden, down_rows, preferred_element_type=jnp.float32)]
    gather x2 -> x1, local copies, waits for them, and re-layouts: 5.55 us -> 1.29 us  [on_device(): clusters[jnp.clip(others, 0, experts - 1)] == clusters[position]]
  transfers between devices with their start and end apart: 10 -> 2, of which waited for: 7 -> 1; matrix products, arithmetic and copies ran while one was open for 9% -> 0% of each run, Pallas kernels for 11% -> 14%
where the time goes in v2:
time: 250 us; the launch traced here: 248 us
  Pallas kernels  149 us (60%)
  matrix products  39.8 us (16%)
  waiting for transfers between devices  29 us (12%)
  starting transfers between devices  18.5 us (7%)
  local copies, waits for them, and re-layouts  6.37 us (3%)
  other arithmetic  5.4 us (2%)
    pallas_call x1, Pallas kernels, inverse_and_sums(): pl.pallas_call(factor_kernel, out_shape=[jax.ShapeDtypeStruct((size, size...  66.7 us
    pallas_call x1, Pallas kernels, cluster_sum(): pl.pallas_call(cluster_kernel, out_shape=jax.ShapeDtypeStruct((rows, rank...  46.3 us
    pallas_call x1, Pallas kernels, gram_sum(): pl.pallas_call(gram_kernel, out_shape=[jax.ShapeDtypeStruct((size, size),...  35.9 us
    all_to_all x1, waiting for transfers between devices, on_device(): lax.all_to_all(answers, 'expert', split_axis=0, concat_axis=0, tiled=True)  29 us
    all_to_all x1, starting transfers between devices, on_device(): lax.all_to_all(answers, 'expert', split_axis=0, concat_axis=0, tiled=True)  10.3 us
    dot_general x2, matrix products, on_device(): jnp.dot(hidden, down_rows, preferred_element_type=jnp.float32)  9.01 us
    all_to_all x1, starting transfers between devices, on_device(): lax.all_to_all(outgoing, 'expert', split_axis=0, concat_axis=0, tiled=True)  8.15 us
    dot_general x2, matrix products, on_device(): jnp.dot(projected, gate_coeff, preferred_element_type=jnp.float32)  6.67 us
  transfers between devices with their start and end apart: 2, of which 1 were waited for; matrix products, arithmetic and copies ran while one was open for 0% of the time, Pallas kernels for 14%

profile of v2, /device:TPU:6, one launch (start us, length us, event | category | flops | bytes accessed | tf_op | source)
XLA Modules:
  0.0 248.2 jit_solution(16013108057466139938)
XLA Ops:
  2.0 1.3 gather_fusion
  3.3 1.3 and_convert_fusion
  4.6 2.0 fusion.14
  6.7 1.9 convolution_add_fusion.part_ref
  9.2 46.3 %shard_map.91 = bf16[896,512]{1,0:T(8,128)(2,1)} custom-call(f32[896,512]{1,0:T(8,128)} %convolution_add_fusion.part_ref, f32[8,512]{1,0:T(8,128)} %broadcast_in_dim.47.weight_ref), custom_call_target="tpu_custom_call" | custom-call | flops 10000000000 | bytes 3670016 | tf_op jit(solution)/shard_map/pallas_call | solution.py:160
  55.5 1.5 copy.18
  57.1 1.5 fusion.6
  58.6 1.5 fusion.5
  61.9 1.6 convolution_convert_fusion
  64.6 8.2 %all-to-all-start = ((bf16[32,24,896]{2,1,0:T(8,128)(2,1)}), bf16[32,24,896]{2,1,0:T(8,128)(2,1)S(1)}, u32[]{:S(2)}, u32[]{:S(2)}) async-start(bf16[32,24,896]{2,1,0:T(8,128)(2,1)} %bitcast.10), calls=%async_computation | async-start | bytes 2752512 | tf_op jit(solution)/shard_map/all_to_all | solution.py:456
  72.8 35.9 %shard_map.92 = (f32[512,512]{1,0:T(8,128)}, bf16[512,896]{1,0:T(8,128)(2,1)}) custom-call(f32[8,64,256]{2,1,0:T(8,128)} %bitcast.111, bf16[512,896]{1,0:T(8,128)(2,1)} %bitcast.109), custom_call_target="tpu_custom_call" | custom-call | flops 40000000000 | bytes 2097152 | tf_op jit(solution)/shard_map/pallas_call | solution.py:251
  108.7 1.9 convolution_convert_fusion.1
  110.6 66.7 %shard_map.93 = (f32[512,512]{1,0:T(8,128)}, bf16[2,2,8,64,512]{4,3,2,1,0:T(8,128)(2,1)}, bf16[2,8,48,512]{3,2,1,0:T(8,128)(2,1)}) custom-call(f32[512,512]{1,0:T(8,128)} %get-tuple-element.18.gram_ref, bf16[2,8,64,512]{3,2,1,0:T(8,128)(2,1)} %pad_maximum_fusion.coeff_ref, bf16[2,8,48,512]{3,2,1,0:T(8,128)(2,1)} %bitcast.110), custom_call_target="tpu_custom_call" | custom-call | flops 40000000000 | bytes 2097152 | tf_op jit(solution)/shard_map/pallas_call | solution.py:379
  177.3 2.0 subtract_convert_fusion
  181.4 1.4 fusion.45
  182.8 1.4 fusion.46
  186.5 1.5 fusion.43
  188.0 3.3 %fusion.7 = f32[768,512]{1,0:T(8,128)} fusion(bf16[768,512]{1,0:T(8,128)(2,1)S(1)} %add_convert_fusion.1, f32[512,512]{1,0:T(8,128)} %fusion.45, bf16[512,512]{1,0:T(8,128)(2,1)S(1)} %get-tuple-element.25, bf16[512,512]{1,0:T(8,128)(2,1)S(1)} %bitcast.95), kind=kOutput, calls=%fused_computation.21 | convolution fusion | flops 671612928 | bytes 4456448 | tf_op jit(solution)/shard_map/dot_general | solution.py:468
  191.3 3.4 %fusion.8 = f32[768,512]{1,0:T(8,128)} fusion(bf16[768,512]{1,0:T(8,128)(2,1)S(1)} %add_convert_fusion.1, f32[512,512]{1,0:T(8,128)} %fusion.43, bf16[512,512]{1,0:T(8,128)(2,1)S(1)} %get-tuple-element.25, bf16[512,512]{1,0:T(8,128)(2,1)S(1)} %bitcast.93), kind=kOutput, calls=%fused_computation.22 | convolution fusion | flops 671612928 | bytes 4456448 | tf_op jit(solution)/shard_map/dot_general | solution.py:468
  194.7 3.7 %multiply_convert_fusion = bf16[768,512]{1,0:T(8,128)(2,1)} fusion(f32[768,512]{1,0:T(8,128)} %fusion.7, bf16[768,512]{1,0:T(8,128)(2,1)S(1)} %add_convert_fusion.1, f32[512,512]{1,0:T(8,128)} %fusion.46, bf16[512,512]{1,0:T(8,128)(2,1)S(1)} %get-tuple-element.25, bf16[512,512]{1,0:T(8,128)(2,1)S(1)} %bitcast.101), kind=kOutput, calls=%fused_computation.3 | convolution fusion | flops 673972224 | bytes 5242880 | tf_op jit(solution)/shard_map/dot_general | solution.py:469
  198.3 4.9 %fusion = f32[768,896]{1,0:T(8,128)} fusion(f32[768,512]{1,0:T(8,128)} %fusion.8, bf16[768,512]{1,0:T(8,128)(2,1)S(1)} %add_convert_fusion.1, bf16[512,512]{1,0:T(8,128)(2,1)} %fusion.2, bf16[1,512,896]{2,1,0:T(8,128)(2,1)} %param.12), kind=kOutput, calls=%fused_computation.12 | convolution fusion | flops 1109655552 | bytes 6553600 | tf_op jit(solution)/shard_map/dot_general | solution.py:471
  203.2 4.1 %add_convert_fusion = bf16[768,896]{1,0:T(8,128)(2,1)} fusion(f32[768,896]{1,0:T(8,128)} %fusion, bf16[768,512]{1,0:T(8,128)(2,1)} %multiply_convert_fusion, bf16[512,896]{1,0:T(8,128)(2,1)S(1)} %copy-done.8), kind=kOutput, calls=%fused_computation.1 | convolution fusion | flops 706019328 | bytes 5832704 | tf_op jit(solution)/shard_map/dot_general | solution.py:471
  207.4 10.3 %all-to-all-start.1 = ((bf16[32,24,896]{2,1,0:T(8,128)(2,1)}), bf16[32,24,896]{2,1,0:T(8,128)(2,1)S(1)}, u32[]{:S(2)}, u32[]{:S(2)}) async-start(bf16[32,24,896]{2,1,0:T(8,128)(2,1)} %bitcast.91), calls=%async_computation.1 | async-start | bytes 2752512 | tf_op jit(solution)/shard_map/all_to_all | solution.py:473
  217.8 29.0 %all-to-all-done.1 = bf16[32,24,896]{2,1,0:T(8,128)(2,1)S(1)} async-done(((bf16[32,24,896]{2,1,0:T(8,128)(2,1)}), bf16[32,24,896]{2,1,0:T(8,128)(2,1)S(1)}, u32[]{:S(2)}, u32[]{:S(2)}) %all-to-all-start.1) | async-done | bytes 1376288 | tf_op jit(solution)/shard_map/all_to_all | solution.py:473
  (48 shorter events, 11.4 us)
Async XLA Ops:
  0.0 6.6 %copy-start = (bf16[1,896,512]{2,1,0:T(8,128)(2,1)S(1)}, bf16[1,896,512]{2,1,0:T(8,128)(2,1)}, u32[]{:S(2)}) copy-start(bf16[1,896,512]{2,1,0:T(8,128)(2,1)} %param.11) | copy-start | bytes 2752516
  4.6 2.1 copy-start.5
  57.1 1.5 copy-start.7
  58.6 1.5 copy-start.12
  58.6 1.8 copy-start.6
  60.1 1.8 copy-start.11
  60.4 3.1 %copy-start.9 = (bf16[1,8,64,512]{3,2,1,0:T(8,128)(2,1)S(1)}, bf16[1,8,64,512]{3,2,1,0:T(8,128)(2,1)}, u32[]{:S(2)}) copy-start(bf16[1,8,64,512]{3,2,1,0:T(8,128)(2,1)} %fusion.6) | copy-start | bytes 1572868
  60.4 3.1 %copy-start.10 = (bf16[1,8,64,512]{3,2,1,0:T(8,128)(2,1)S(1)}, bf16[1,8,64,512]{3,2,1,0:T(8,128)(2,1)}, u32[]{:S(2)}) copy-start(bf16[1,8,64,512]{3,2,1,0:T(8,128)(2,1)} %fusion.5) | copy-start | bytes 1572868
  64.6 44.1 %all-to-all-start = ((bf16[32,24,896]{2,1,0:T(8,128)(2,1)}), bf16[32,24,896]{2,1,0:T(8,128)(2,1)S(1)}, u32[]{:S(2)}, u32[]{:S(2)}) async-start(bf16[32,24,896]{2,1,0:T(8,128)(2,1)} %bitcast.10), calls=%async_computation | async-start | bytes 2752512 | tf_op jit(solution)/shard_map/all_to_all | solution.py:456
  177.3 2.2 copy-start.2
  179.5 1.3 copy-start.1
  179.7 3.1 %copy-start.3 = (bf16[1,1,8,64,512]{4,3,2,1,0:T(8,128)(2,1)}, bf16[1,1,8,64,512]{4,3,2,1,0:T(8,128)(2,1)S(1)}, u32[]{:S(2)}) copy-start(bf16[1,1,8,64,512]{4,3,2,1,0:T(8,128)(2,1)S(1)} %get-tuple-element.27) | copy-start | bytes 1572868
  191.3 3.4 %copy-start.4 = (bf16[1,1,8,64,512]{4,3,2,1,0:T(8,128)(2,1)S(1)}, bf16[1,1,8,64,512]{4,3,2,1,0:T(8,128)(2,1)}, u32[]{:S(2)}) copy-start(bf16[1,1,8,64,512]{4,3,2,1,0:T(8,128)(2,1)} %copy-done.3) | copy-start | bytes 1572868
  198.3 4.9 %copy-start.8 = (bf16[512,896]{1,0:T(8,128)(2,1)S(1)}, bf16[512,896]{1,0:T(8,128)(2,1)}, u32[]{:S(2)}) copy-start(bf16[512,896]{1,0:T(8,128)(2,1)} %get-tuple-element.24) | copy-start | bytes 2752516
  207.4 10.3 %copy-start.13 = (f32[64,8]{0,1:T(8,128)S(1)}, f32[64,8]{0,1:T(8,128)}, u32[]{:S(2)}) copy-start(f32[64,8]{0,1:T(8,128)} %param.16) | copy-start | bytes 6148
  207.4 39.4 %all-to-all-start.1 = ((bf16[32,24,896]{2,1,0:T(8,128)(2,1)}), bf16[32,24,896]{2,1,0:T(8,128)(2,1)S(1)}, u32[]{:S(2)}, u32[]{:S(2)}) async-start(bf16[32,24,896]{2,1,0:T(8,128)(2,1)} %bitcast.91), calls=%async_computation.1 | async-start | bytes 2752512 | tf_op jit(solution)/shard_map/all_to_all | solution.py:473

commit v3 on v2

--- a/solution.py
+++ b/solution.py
@@ -44,8 +44,8 @@
                 c2 = jnp.broadcast_to(old[:, k + 1:k + 2], (8, BLK))
                 new = jnp.where(both, 0.0, old) - c1 * v1 - c2 * v2
             tiles[i] = new
-        if k % 32 == 30:
-            serve(k // 32)
+        if k % 16 == 14:
+            serve(k // 16)
     return [jnp.where(lane <= sub + 8 * i, tiles[i], 0.0) for i in range(n)]
 
 def eliminate(out_ref, inv_ref, serve):
@@ -55,7 +55,7 @@
     def step(j, carry):
         at = pl.multiple_of(j * BLK, BLK)
         tiles = [out_ref[pl.ds(pl.multiple_of(at + 8 * i, 8), 8), pl.ds(at, BLK)] for i in range(BLK // 8)]
-        for i, tile in enumerate(factor_block(tiles, lambda turn: serve(4 * j + turn))):
+        for i, tile in enumerate(factor_block(tiles, lambda turn: serve(turn % 2, 4 * j + turn // 2))):
             inv_ref[8 * i:8 * i + 8, :] = tile
         inv = inv_ref[...]
         rows = lax.broadcasted_iota(jnp.int32, (BLK, BLK), 0)
@@ -82,7 +82,7 @@
 CUTS = 4
 
 
-def cluster_kernel(part_ref, weight_ref, out_ref, stage, got, own, plus, minus, acc,
+def cluster_kernel(part_ref, cluster_ref, out_ref, stage, got, own, plus, minus, acc,
                    dp_send, dp_recv, up_send, up_recv, low_send, low_recv, fin_send, fin_recv):
     count = lax.axis_size("expert")
     me = lax.axis_index("expert")
@@ -92,6 +92,14 @@
     before = {"expert": lax.rem(me + count - 1, count)}
     part = part_ref.shape[0] // 2
     size = part // CUTS
+    mine = cluster_ref[me]
+
+    def share(step):
+        other = me + step
+        inside = jnp.logical_and(other >= 0, other < count)
+        same = cluster_ref[lax.rem(other + count, count)] == mine
+        return jnp.where(jnp.logical_and(inside, same), 1.0, 0.0).astype(jnp.float32)
+
     barrier = pltpu.get_barrier_semaphore()
     for device in (sibling, after, before):
         pl.semaphore_signal(barrier, inc=1, device_id=device, device_id_type=MESH)
@@ -138,8 +146,8 @@
             back(hop, cut).wait_recv()
             if hop < REACH - 1:
                 back(hop + 1, cut).start()
-            total = acc[cut] + weight_ref[hop:hop + 1, :] * plus[hop, cut].astype(jnp.float32)
-            total = total + weight_ref[REACH + hop:REACH + hop + 1, :] * minus[hop, cut].astype(jnp.float32)
+            total = acc[cut] + share(-1 - hop) * plus[hop, cut].astype(jnp.float32)
+            total = total + share(hop + 1) * minus[hop, cut].astype(jnp.float32)
             if hop < REACH - 1:
                 acc[cut] = total
             else:
@@ -154,13 +162,13 @@
             back(hop, cut).wait_send()
 
 
-def cluster_sum(sketched, weights):
+def cluster_sum(sketched, clusters):
     rows, rank = sketched.shape
     size = rows // 2 // CUTS
     return pl.pallas_call(
         cluster_kernel,
         out_shape=jax.ShapeDtypeStruct((rows, rank), jnp.bfloat16),
-        in_specs=[pl.BlockSpec(memory_space=pltpu.VMEM)] * 2,
+        in_specs=[pl.BlockSpec(memory_space=pltpu.VMEM), pl.BlockSpec(memory_space=pltpu.SMEM)],
         out_specs=pl.BlockSpec(memory_space=pltpu.VMEM),
         scratch_shapes=[
             pltpu.VMEM((CUTS, size, rank), jnp.bfloat16),
@@ -180,7 +188,7 @@
         ],
         compiler_params=pltpu.CompilerParams(collective_id=3, has_side_effects=True),
         cost_estimate=pl.CostEstimate(flops=10 ** 10, bytes_accessed=8 * rows * rank, transcendentals=0),
-    )(sketched, weights)
+    )(sketched, clusters)
 
 
 def gram_kernel(part_ref, down_ref, out_ref, other_ref, arrive, pieces, rs_send, rs_recv, ag_send, ag_recv, sib_send, sib_recv, down_send, down_recv):
@@ -262,7 +270,7 @@
     )(part, down)
 
 
-def factor_kernel(gram_ref, coeff_ref, raw_ref, out_ref, coeff_all, raw_all, inv_ref, coeff_slot, raw_slot,
+def factor_kernel(gram_ref, coeff_ref, raw_ref, high_ref, low_ref, coeff_all, raw_all, out_ref, inv_ref, coeff_slot, raw_slot,
                   send, recv, sib_send, sib_recv):
     count = coeff_ref.shape[1]
     hops = count - 1
@@ -309,10 +317,10 @@
     for kind, side in both:
         first(kind, side).start()
 
-    def serve(turn):
+    def serve(kind, turn):
         @pl.when(turn < hops)
         def _():
-            for kind, side in both:
+            for side in range(2):
                 slot = (coeff_slot, raw_slot)[kind]
                 remote(slot.at[side, turn], slot.at[side, turn], kind, side, turn).wait_recv()
                 part = (coeff_ref, raw_ref)[kind][side, chunk(side, turn + 2)]
@@ -332,7 +340,7 @@
 
         @pl.when((turn >= hops) & (turn < 2 * hops))
         def _():
-            for kind, side in both:
+            for side in range(2):
                 here = place(kind, side, chunk(side, turn - hops + 1))
                 remote(here, here, kind, side, turn).wait_recv()
 
@@ -345,6 +353,9 @@
 
     out_ref[...] = gram_ref[...]
     eliminate(out_ref, inv_ref, serve)
+    high = out_ref[...].astype(jnp.bfloat16)
+    high_ref[...] = high
+    low_ref[...] = (out_ref[...] - high.astype(jnp.float32)).astype(jnp.bfloat16)
 
     for kind, side in both:
         first(kind, side).wait_send()
@@ -379,13 +390,15 @@
     return pl.pallas_call(
         factor_kernel,
         out_shape=[
-            jax.ShapeDtypeStruct((size, size), jnp.float32),
+            jax.ShapeDtypeStruct((size, size), jnp.bfloat16),
+            jax.ShapeDtypeStruct((size, size), jnp.bfloat16),
             jax.ShapeDtypeStruct((2,) + coeff.shape, jnp.bfloat16),
             jax.ShapeDtypeStruct(raw.shape, jnp.bfloat16),
         ],
         in_specs=[pl.BlockSpec(memory_space=pltpu.VMEM)] * 3,
-        out_specs=[pl.BlockSpec(memory_space=pltpu.VMEM)] * 3,
+        out_specs=[pl.BlockSpec(memory_space=pltpu.VMEM)] * 4,
         scratch_shapes=[
+            pltpu.VMEM((size, size), jnp.float32),
             pltpu.VMEM((BLK, BLK), jnp.float32),
             pltpu.VMEM(slots(coeff), jnp.bfloat16),
             pltpu.VMEM(slots(raw), jnp.bfloat16),
@@ -399,16 +412,93 @@
     )(gram, coeff, raw)
 
 
-def split_dot(precise, plain, transposed):
-    high = precise.astype(jnp.bfloat16)
-    low = (precise - high.astype(jnp.float32)).astype(jnp.bfloat16)
-    if transposed:
-        dims = (((1,), (1,)), ((), ()))
-        return lax.dot_general(plain, high, dims, preferred_element_type=jnp.float32) + lax.dot_general(
-            plain, low, dims, preferred_element_type=jnp.float32)
-    dims = (((1,), (0,)), ((), ()))
-    return lax.dot_general(high, plain, dims, preferred_element_type=jnp.float32) + lax.dot_general(
-        low, plain, dims, preferred_element_type=jnp.float32)
+GROUP = 8
+
+
+def expert_kernel(high_ref, low_ref, coeff_ref, raw_ref, down_ref, other_ref, back_ref, final, answers, send, recv):
+    count, capacity, width = back_ref.shape
+    me = lax.axis_index("expert")
+    span = GROUP * capacity
+    groups = count // GROUP
+    barrier = pltpu.get_barrier_semaphore()
+
+    def greet(step, carry):
+        pl.semaphore_signal(barrier, inc=1, device_id={"expert": lax.rem(me + step, count)}, device_id_type=MESH)
+        return carry
+
+    lax.fori_loop(1, count, greet, 0)
+    high = high_ref[...]
+    low = low_ref[...]
+    for index in range(4):
+        block = coeff_ref[index]
+        final[index] = (jnp.dot(high, block, preferred_element_type=jnp.float32)
+                        + jnp.dot(low, block, preferred_element_type=jnp.float32)).astype(jnp.bfloat16)
+    pl.semaphore_wait(barrier, count - 1)
+
+    def give(target):
+        return pltpu.make_async_remote_copy(
+            src_ref=answers.at[target], dst_ref=back_ref.at[me], send_sem=send.at[target], recv_sem=recv.at[me],
+            device_id={"expert": target}, device_id_type=MESH)
+
+    def take(source):
+        return pltpu.make_async_remote_copy(
+            src_ref=back_ref.at[source], dst_ref=back_ref.at[source], send_sem=send.at[source], recv_sem=recv.at[source],
+            device_id={"expert": source}, device_id_type=MESH)
+
+    dims = (((1,), (1,)), ((), ()))
+
+    def compute(turn, carry):
+        group = lax.rem(me // GROUP + turn, groups)
+        rows = raw_ref[pl.ds(pl.multiple_of(group * span, 16), span), :]
+        projected = (lax.dot_general(rows, high_ref[...], dims, preferred_element_type=jnp.float32)
+                     + lax.dot_general(rows, low_ref[...], dims, preferred_element_type=jnp.float32)).astype(jnp.bfloat16)
+        total = jnp.zeros((span, width), jnp.float32)
+        for side, rows_ref in enumerate((down_ref, other_ref)):
+            gate = jnp.dot(projected, final[2 * side], preferred_element_type=jnp.float32)
+            up = jnp.dot(projected, final[2 * side + 1], preferred_element_type=jnp.float32)
+            hidden = (gate / (1.0 + jnp.exp(-gate)) * up).astype(jnp.bfloat16)
+            total = total + jnp.dot(hidden, rows_ref[...], preferred_element_type=jnp.float32)
+        for index in range(GROUP):
+            target = group * GROUP + index
+            value = total[index * capacity:(index + 1) * capacity].astype(jnp.bfloat16)
+
+            @pl.when(target == me)
+            def _():
+                back_ref[me] = value
+
+            @pl.when(target != me)
+            def _():
+                answers[target] = value
+                give(target).start()
+        return carry
+
+    lax.fori_loop(0, groups, compute, 0)
+
+    def drain(step, carry):
+        take(lax.rem(me + step, count)).wait_recv()
+        give(lax.rem(me + step, count)).wait_send()
+        return carry
+
+    lax.fori_loop(1, count, drain, 0)
+
+
+def expert_answers(high, low, coeff, raw, down, other, count, capacity):
+    rank = high.shape[0]
+    width = down.shape[1]
+    return pl.pallas_call(
+        expert_kernel,
+        out_shape=jax.ShapeDtypeStruct((count, capacity, width), jnp.bfloat16),
+        in_specs=[pl.BlockSpec(memory_space=pltpu.VMEM)] * 6,
+        out_specs=pl.BlockSpec(memory_space=pltpu.VMEM),
+        scratch_shapes=[
+            pltpu.VMEM((4, rank, rank), jnp.bfloat16),
+            pltpu.VMEM((count, capacity, width), jnp.bfloat16),
+            pltpu.SemaphoreType.DMA((count,)),
+            pltpu.SemaphoreType.DMA((count,)),
+        ],
+        compiler_params=pltpu.CompilerParams(collective_id=4, has_side_effects=True),
+        cost_estimate=pl.CostEstimate(flops=20 * 10 ** 9, bytes_accessed=8 * rank * rank, transcendentals=0),
+    )(high, low, coeff, raw, down, other)
 
 
 def transposed_dot(left, right):
@@ -421,18 +511,12 @@
     experts = lax.axis_size("expert")
     tensors = lax.axis_size("tensor")
     half = lax.axis_index("dp")
-    position = lax.axis_index("expert")
     sketched = jnp.dot(gate_rows, sketch[0, 0], preferred_element_type=jnp.float32) + jnp.dot(
         up_rows, sketch[0, 1], preferred_element_type=jnp.float32
     )
     rank = sketched.shape[1]
 
-    offsets = jnp.array([-1, -2, -3, 1, 2, 3, 0, 0], jnp.int32)
-    others = position + offsets
-    inside = (others >= 0) & (others < experts)
-    same = inside & (clusters[jnp.clip(others, 0, experts - 1)] == clusters[position])
-    weights = jnp.broadcast_to(same.astype(jnp.float32)[:, None], (8, rank))
-    summed = cluster_sum(sketched, weights)
+    summed = cluster_sum(sketched, clusters)
 
     tok_rows, width = tokens.shape
     top_count = routes.shape[1]
@@ -458,19 +542,10 @@
     arrived, gram = lax.optimization_barrier((arrived, gram))
     raw = jnp.dot(arrived.reshape(experts * capacity, width), summed, preferred_element_type=jnp.float32)
     raw = raw.astype(jnp.bfloat16).reshape(2, tensors, experts * capacity // (2 * tensors), rank)
-    inverse, coeff, raw = inverse_and_sums(gram, coeff, raw)
-
-    projected = split_dot(inverse, raw.reshape(experts * capacity, rank), True).astype(jnp.bfloat16)
-    answers = 0.0
-    for index, down_rows in enumerate((down_weight[0], down_other)):
-        gate_coeff = split_dot(inverse, coeff[index, 0].reshape(rank, -1), False).astype(jnp.bfloat16)
-        up_coeff = split_dot(inverse, coeff[index, 1].reshape(rank, -1), False).astype(jnp.bfloat16)
-        gate_part = jnp.dot(projected, gate_coeff, preferred_element_type=jnp.float32)
-        up_part = jnp.dot(projected, up_coeff, preferred_element_type=jnp.float32)
-        hidden = (jax.nn.silu(gate_part) * up_part).astype(jnp.bfloat16)
-        answers = answers + jnp.dot(hidden, down_rows, preferred_element_type=jnp.float32)
-    answers = answers.astype(jnp.bfloat16).reshape(experts, capacity, width)
-    returned = lax.all_to_all(answers, "expert", split_axis=0, concat_axis=0, tiled=True)
+    high, low, coeff, raw = inverse_and_sums(gram, coeff, raw)
+    returned = expert_answers(
+        high, low, coeff.reshape(4, rank, -1), raw.reshape(experts * capacity, rank),
+        down_weight[0], down_other, experts, capacity)
     returned = returned.reshape(experts * capacity, width)
     mixing = jnp.where(holds, shares[:, None, :], 0.0).reshape(experts * capacity, tok_rows)
     high = mixing.astype(jnp.bfloat16)

time: 250 us -> 220 us (0.88)
  Pallas kernels: 149 us -> 191 us
  waiting for transfers between devices: 29 us -> 0.01 us
  matrix products: 39.8 us -> 14.9 us
  starting transfers between devices: 18.5 us -> 8.28 us
  other arithmetic: 5.4 us -> 1.34 us
  local copies, waits for them, and re-layouts: 6.37 us -> 3.77 us
    pallas_call x0 -> x1, Pallas kernels: none -> 40 us  [expert_answers(): pl.pallas_call(expert_kernel, out_shape=jax.ShapeDtypeStruct((count, capa...]
    all_to_all x1 -> x0, waiting for transfers between devices: 29 us -> none  [on_device(): lax.all_to_all(answers, 'expert', split_axis=0, concat_axis=0, tiled=True)]
    dot_general x12 -> x0, matrix products: 26.5 us -> none  [the longest x2 9.01 us: on_device(): jnp.dot(hidden, down_rows, preferred_element_type=jnp.float32)]
    all_to_all x1 -> x0, starting transfers between devices: 10.3 us -> none  [on_device(): lax.all_to_all(answers, 'expert', split_axis=0, concat_axis=0, tiled=True)]
    convert_element_type x2 -> x0, other arithmetic: 3.28 us -> none  [the longest x1 1.96 us: split_dot(): low = (precise - high.astype(jnp.float32)).astype(jnp.bfloat16)]
  transfers between devices with their start and end apart: 2 -> 1, of which waited for: 1 -> 0; matrix products, arithmetic and copies ran while one was open for 0% -> 0% of each run, Pallas kernels for 14% -> 16%
where the time goes in v3:
time: 220 us; the launch traced here: 219 us
  Pallas kernels  191 us (87%)
  matrix products  14.9 us (7%)
  starting transfers between devices  8.28 us (4%)
  local copies, waits for them, and re-layouts  3.77 us (2%)
    pallas_call x1, Pallas kernels, inverse_and_sums(): pl.pallas_call(factor_kernel, out_shape=[jax.ShapeDtypeStruct((size, size...  68.6 us
    pallas_call x1, Pallas kernels, cluster_sum(): pl.pallas_call(cluster_kernel, out_shape=jax.ShapeDtypeStruct((rows, rank...  46.3 us
    pallas_call x1, Pallas kernels, expert_answers(): pl.pallas_call(expert_kernel, out_shape=jax.ShapeDtypeStruct((count, capa...  40 us
    pallas_call x1, Pallas kernels, gram_sum(): pl.pallas_call(gram_kernel, out_shape=[jax.ShapeDtypeStruct((size, size),...  36 us
    all_to_all x1, starting transfers between devices, on_device(): lax.all_to_all(outgoing, 'expert', split_axis=0, concat_axis=0, tiled=True)  8.28 us
    dot_general x5, matrix products, transposed_dot(): lax.dot_general(left, right, (((0,), (0,)), ((), ())), preferred_element_...  7.61 us
  transfers between devices with their start and end apart: 1, of which 0 were waited for; matrix products, arithmetic and copies ran while one was open for 0% of the time, Pallas kernels for 16%

profile of v3, /device:TPU:6, one launch (start us, length us, event | category | flops | bytes accessed | tf_op | source)
XLA Modules:
  0.0 219.3 jit_solution(7360954609174725051)
XLA Ops:
  0.0 1.2 copy-done
  1.2 1.8 fusion.7
  3.0 1.9 convolution_add_fusion.part_ref
  4.9 46.3 %shard_map.82 = bf16[896,512]{1,0:T(8,128)(2,1)} custom-call(f32[896,512]{1,0:T(8,128)} %convolution_add_fusion.part_ref, s32[32]{0:T(128)} %cluster_ref.1), custom_call_target="tpu_custom_call" | custom-call | flops 10000000000 | bytes 3670016 | tf_op jit(solution)/shard_map/pallas_call | solution.py:168
  51.2 1.5 copy.18
  52.8 0.9 copy-done.5
  53.7 0.7 fusion
  54.4 0.0 copy-start.8
  54.5 2.8 %fusion.1 = bf16[1,8,64,512]{3,2,1,0:T(8,128)(2,1)} fusion(bf16[8,64,896]{2,1,0:T(8,128)(2,1)} %bitcast.60, bf16[1,896,512]{2,1,0:T(8,128)(2,1)S(1)} %copy-done.3), kind=kOutput, calls=%fused_computation.6 | convolution fusion | flops 470024192 | bytes 2359296 | tf_op jit(solution)/shard_map/dot_general | solution.py:505
  57.2 0.1 fusion.27
  57.3 0.1 convolution_convert_fusion.4
  57.4 0.1 eq.48
  57.5 1.3 fusion.13
  58.8 0.2 fusion.17
  59.0 1.6 convolution_convert_fusion
  60.6 1.1 pad_maximum_fusion.coeff_ref
  61.7 8.3 %all-to-all-start = ((bf16[32,24,896]{2,1,0:T(8,128)(2,1)}), bf16[32,24,896]{2,1,0:T(8,128)(2,1)S(1)}, u32[]{:S(2)}, u32[]{:S(2)}) async-start(bf16[32,24,896]{2,1,0:T(8,128)(2,1)} %bitcast.9), calls=%async_computation | async-start | bytes 2752512 | tf_op jit(solution)/shard_map/all_to_all | solution.py:540
  70.0 36.0 %shard_map.83 = (f32[512,512]{1,0:T(8,128)}, bf16[512,896]{1,0:T(8,128)(2,1)}) custom-call(f32[8,64,256]{2,1,0:T(8,128)} %bitcast.69, bf16[512,896]{1,0:T(8,128)(2,1)} %bitcast.64), custom_call_target="tpu_custom_call" | custom-call | flops 40000000000 | bytes 2097152 | tf_op jit(solution)/shard_map/pallas_call | solution.py:259
  106.0 0.0 all-to-all-done
  106.0 1.9 convolution_convert_fusion.1
  107.9 68.6 %shard_map.84 = (bf16[512,512]{1,0:T(8,128)(2,1)}, bf16[512,512]{1,0:T(8,128)(2,1)}, bf16[2,2,8,64,512]{4,3,2,1,0:T(8,128)(2,1)}, bf16[2,8,48,512]{3,2,1,0:T(8,128)(2,1)}) custom-call(f32[512,512]{1,0:T(8,128)} %get-tuple-element.19.gram_ref, bf16[2,8,64,512]{3,2,1,0:T(8,128)(2,1)} %pad_maximum_fusion.coeff_ref, bf16[2,8,48,512]{3,2,1,0:T(8,128)(2,1)} %bitcast.68), custom_call_target="tpu_custom_call" | custom-call | flops 40000000000 | bytes 2097152 | tf_op jit(solution)/shard_map/pallas_call | solution.py:390
  176.5 40.0 %shard_map.85 = bf16[32,24,896]{2,1,0:T(8,128)(2,1)} custom-call(bf16[512,512]{1,0:T(8,128)(2,1)} %get-tuple-element.22.high_ref, bf16[512,512]{1,0:T(8,128)(2,1)} %get-tuple-element.23.low_ref, bf16[4,512,512]{2,1,0:T(8,128)(2,1)} %bitcast.66, bf16[768,512]{1,0:T(8,128)(2,1)} %bitcast.67, bf16[512,896]{1,0:T(8,128)(2,1)} %bitcast.65, ...), custom_call_target="tpu_custom_call" | custom-call | flops 20000000000 | bytes 2097152 | tf_op jit(solution)/shard_map/pallas_call | solution.py:488
  216.5 1.8 convolution_bitcast_fusion.1
  218.3 1.0 fusion.3
  (19 shorter events, 0.1 us)
Async XLA Ops:
  0.0 1.2 copy-start
  1.2 1.8 copy-start.2
  1.2 1.8 copy-start.3
  52.8 0.9 copy-start.5
  54.4 2.8 %copy-start.8 = (s32[64,8]{0,1:T(8,128)S(1)}, s32[64,8]{0,1:T(8,128)}, u32[]{:S(2)}) copy-start(s32[64,8]{0,1:T(8,128)} %param.14) | copy-start | bytes 6148
  54.4 3.1 %copy-start.4 = (bf16[896,512]{1,0:T(8,128)(2,1)S(1)}, bf16[896,512]{1,0:T(8,128)(2,1)}, u32[]{:S(2)}) copy-start(bf16[896,512]{1,0:T(8,128)(2,1)} %shard_map.82) | copy-start | bytes 2752516
  57.2 1.8 copy-start.7
  57.5 3.1 %copy-start.6 = (bf16[1,8,64,512]{3,2,1,0:T(8,128)(2,1)S(1)}, bf16[1,8,64,512]{3,2,1,0:T(8,128)(2,1)}, u32[]{:S(2)}) copy-start(bf16[1,8,64,512]{3,2,1,0:T(8,128)(2,1)} %fusion.1) | copy-start | bytes 1572868
  61.7 8.3 %copy-start.9 = (f32[64,8]{0,1:T(8,128)S(1)}, f32[64,8]{0,1:T(8,128)}, u32[]{:S(2)}) copy-start(f32[64,8]{0,1:T(8,128)} %param.15) | copy-start | bytes 6148
  61.7 44.3 %all-to-all-start = ((bf16[32,24,896]{2,1,0:T(8,128)(2,1)}), bf16[32,24,896]{2,1,0:T(8,128)(2,1)S(1)}, u32[]{:S(2)}, u32[]{:S(2)}) async-start(bf16[32,24,896]{2,1,0:T(8,128)(2,1)} %bitcast.9), calls=%async_computation | async-start | bytes 2752512 | tf_op jit(solution)/shard_map/all_to_all | solution.py:540
  216.5 1.8 copy-start.1

commit v4 on v3

--- a/solution.py
+++ b/solution.py
@@ -44,8 +44,8 @@
                 c2 = jnp.broadcast_to(old[:, k + 1:k + 2], (8, BLK))
                 new = jnp.where(both, 0.0, old) - c1 * v1 - c2 * v2
             tiles[i] = new
-        if k % 16 == 14:
-            serve(k // 16)
+        if k % 32 == 30:
+            serve(k // 32)
     return [jnp.where(lane <= sub + 8 * i, tiles[i], 0.0) for i in range(n)]
 
 def eliminate(out_ref, inv_ref, serve):
@@ -55,7 +55,7 @@
     def step(j, carry):
         at = pl.multiple_of(j * BLK, BLK)
         tiles = [out_ref[pl.ds(pl.multiple_of(at + 8 * i, 8), 8), pl.ds(at, BLK)] for i in range(BLK // 8)]
-        for i, tile in enumerate(factor_block(tiles, lambda turn: serve(turn % 2, 4 * j + turn // 2))):
+        for i, tile in enumerate(factor_block(tiles, lambda turn: serve(turn % 2, 2 * j + turn // 2))):
             inv_ref[8 * i:8 * i + 8, :] = tile
         inv = inv_ref[...]
         rows = lax.broadcasted_iota(jnp.int32, (BLK, BLK), 0)
@@ -79,7 +79,7 @@
     out_ref[...] = jnp.where(column <= row, out_ref[...], 0.0)
 
 REACH = 3
-CUTS = 4
+CUTS = 7
 
 
 def cluster_kernel(part_ref, cluster_ref, out_ref, stage, got, own, plus, minus, acc,
@@ -272,84 +272,90 @@
 
 def factor_kernel(gram_ref, coeff_ref, raw_ref, high_ref, low_ref, coeff_all, raw_all, out_ref, inv_ref, coeff_slot, raw_slot,
                   send, recv, sib_send, sib_recv):
-    count = coeff_ref.shape[1]
-    hops = count - 1
+    count = coeff_ref.shape[0]
+    longer = count // 2
+    reach = (longer, longer - 1)
     me = lax.axis_index("tensor")
     half = lax.axis_index("dp")
     sibling = {"dp": 1 - half}
-    neighbours = ({"tensor": lax.rem(me + 1, count)}, {"tensor": lax.rem(me + hops, count)})
+    after = {"tensor": lax.rem(me + 1, count)}
+    before = {"tensor": lax.rem(me + count - 1, count)}
+    parts, slots = (coeff_ref, raw_ref), (coeff_slot, raw_slot)
     barrier = pltpu.get_barrier_semaphore()
-    for device in (sibling,) + neighbours:
+    for device in (sibling, after, before):
         pl.semaphore_signal(barrier, inc=1, device_id=device, device_id_type=MESH)
     pl.semaphore_wait(barrier, 3)
 
-    def chunk(side, distance):
-        return lax.rem(me + (2 * count - distance if side == 0 else distance), count)
-
-    def place(kind, side, index):
-        return coeff_all.at[0, side, index] if kind == 0 else raw_all.at[side, index]
+    def upward(kind, side):
+        return kind == side
+
+    def chunk(kind, side, distance):
+        return lax.rem(me + (distance if upward(kind, side) else count - distance), count)
+
+    def place(kind, index):
+        return coeff_all.at[0, index] if kind == 0 else raw_all.at[index]
 
     def remote(src, dst, kind, side, turn):
         return pltpu.make_async_remote_copy(
             src_ref=src, dst_ref=dst, send_sem=send.at[kind, side, turn], recv_sem=recv.at[kind, side, turn],
-            device_id=neighbours[side], device_id_type=MESH)
+            device_id=after if upward(kind, side) else before, device_id_type=MESH)
 
     def first(kind, side):
-        part = (coeff_ref, raw_ref)[kind].at[side, chunk(side, 1)]
-        return remote(part, (coeff_slot, raw_slot)[kind].at[side, 0], kind, side, 0)
+        return remote(parts[kind].at[chunk(kind, side, reach[side])], slots[kind].at[side, 0], kind, side, 0)
 
     def add_on(kind, side, turn):
-        slot = (coeff_slot, raw_slot)[kind]
-        return remote(slot.at[side, turn - 1], slot.at[side, turn], kind, side, turn)
-
-    def pass_on(kind, side, turn):
-        here = place(kind, side, chunk(side, turn - hops))
-        return remote(here, here, kind, side, turn)
-
-    def share(side, number):
-        index = chunk(side, number)
-        return pltpu.make_async_remote_copy(
-            src_ref=coeff_all.at[0, side, index], dst_ref=coeff_all.at[1, side, index],
-            send_sem=sib_send.at[side, number], recv_sem=sib_recv.at[side, number],
-            device_id=sibling, device_id_type=MESH)
-
-    both = [(kind, side) for kind in range(2) for side in range(2)]
-    for kind, side in both:
-        first(kind, side).start()
+        return remote(slots[kind].at[side, turn - 1], slots[kind].at[side, turn], kind, side, turn)
+
+    def pass_on(kind, side, hop):
+        here = place(kind, lax.rem(me + (count - hop if upward(kind, side) else hop), count))
+        return remote(here, here, kind, side, longer + hop)
+
+    def share(index):
+        return pltpu.make_async_remote_copy(
+            src_ref=coeff_all.at[0, index], dst_ref=coeff_all.at[1, index], send_sem=sib_send.at[index],
+            recv_sem=sib_recv.at[index], device_id=sibling, device_id_type=MESH)
+
+    for kind in range(2):
+        for side in range(2):
+            first(kind, side).start()
 
     def serve(kind, turn):
-        @pl.when(turn < hops)
+        for side in range(2):
+            @pl.when(turn < reach[side])
+            def _():
+                slot = slots[kind].at[side, turn]
+                remote(slot, slot, kind, side, turn).wait_recv()
+
+            @pl.when(turn < reach[side] - 1)
+            def _():
+                part = parts[kind][chunk(kind, side, reach[side] - 1 - turn)]
+                value = slots[kind][side, turn].astype(jnp.float32) + part.astype(jnp.float32)
+                slots[kind][side, turn] = value.astype(jnp.bfloat16)
+                add_on(kind, side, turn + 1).start()
+
+        @pl.when(turn == longer - 1)
         def _():
+            value = parts[kind][me].astype(jnp.float32) + slots[kind][0, longer - 1].astype(jnp.float32)
+            value = value + slots[kind][1, longer - 2].astype(jnp.float32)
+            place(kind, me)[...] = value.astype(jnp.bfloat16)
             for side in range(2):
-                slot = (coeff_slot, raw_slot)[kind]
-                remote(slot.at[side, turn], slot.at[side, turn], kind, side, turn).wait_recv()
-                part = (coeff_ref, raw_ref)[kind][side, chunk(side, turn + 2)]
-                value = (slot[side, turn].astype(jnp.float32) + part.astype(jnp.float32)).astype(jnp.bfloat16)
-
-                @pl.when(turn < hops - 1)
-                def _():
-                    slot[side, turn] = value
-                    add_on(kind, side, turn + 1).start()
-
-                @pl.when(turn == hops - 1)
-                def _():
-                    place(kind, side, me)[...] = value
-                    pass_on(kind, side, turn + 1).start()
-                    if kind == 0:
-                        share(side, 0).start()
-
-        @pl.when((turn >= hops) & (turn < 2 * hops))
-        def _():
-            for side in range(2):
-                here = place(kind, side, chunk(side, turn - hops + 1))
-                remote(here, here, kind, side, turn).wait_recv()
-
-                @pl.when(turn < 2 * hops - 1)
-                def _():
-                    pass_on(kind, side, turn + 1).start()
-
+                pass_on(kind, side, 0).start()
+            if kind == 0:
+                share(me).start()
+
+        hop = turn - longer
+        for side in range(2):
+            index = lax.rem(me + (2 * count - 1 - hop if upward(kind, side) else hop + 1), count)
+
+            @pl.when((hop >= 0) & (hop < reach[side]))
+            def _():
+                remote(place(kind, index), place(kind, index), kind, side, turn).wait_recv()
                 if kind == 0:
-                    share(side, turn - hops + 1).start()
+                    share(index).start()
+
+            @pl.when((hop >= 0) & (hop < reach[side] - 1))
+            def _():
+                pass_on(kind, side, hop + 1).start()
 
     out_ref[...] = gram_ref[...]
     eliminate(out_ref, inv_ref, serve)
@@ -357,26 +363,17 @@
     high_ref[...] = high
     low_ref[...] = (out_ref[...] - high.astype(jnp.float32)).astype(jnp.bfloat16)
 
-    for kind, side in both:
-        first(kind, side).wait_send()
-
-    def drain(turn, carry):
-        for kind, side in both:
-            @pl.when(turn < hops)
-            def _():
+    for kind in range(2):
+        for side in range(2):
+            first(kind, side).wait_send()
+            for turn in range(1, reach[side]):
                 add_on(kind, side, turn).wait_send()
-
-            @pl.when(turn >= hops)
-            def _():
-                pass_on(kind, side, turn).wait_send()
-        return carry
-
-    lax.fori_loop(1, 2 * hops, drain, 0)
-
-    def shared(number, carry):
-        for side in range(2):
-            share(side, number).wait_send()
-            share(side, number).wait_recv()
+            for hop in range(reach[side]):
+                pass_on(kind, side, hop).wait_send()
+
+    def shared(index, carry):
+        share(index).wait_send()
+        share(index).wait_recv()
         return carry
 
     lax.fori_loop(0, count, shared, 0)
@@ -384,9 +381,8 @@
 
 def inverse_and_sums(gram, coeff, raw):
     size = gram.shape[0]
-    count = coeff.shape[1]
-    steps = 2 * (count - 1)
-    slots = lambda array: (2, count - 1) + array.shape[2:]
+    count = coeff.shape[0]
+    slots = lambda array: (2, count // 2) + array.shape[1:]
     return pl.pallas_call(
         factor_kernel,
         out_shape=[
@@ -402,10 +398,10 @@
             pltpu.VMEM((BLK, BLK), jnp.float32),
             pltpu.VMEM(slots(coeff), jnp.bfloat16),
             pltpu.VMEM(slots(raw), jnp.bfloat16),
-            pltpu.SemaphoreType.DMA((2, 2, steps)),
-            pltpu.SemaphoreType.DMA((2, 2, steps)),
-            pltpu.SemaphoreType.DMA((2, count)),
-            pltpu.SemaphoreType.DMA((2, count)),
+            pltpu.SemaphoreType.DMA((2, 2, count)),
+            pltpu.SemaphoreType.DMA((2, 2, count)),
+            pltpu.SemaphoreType.DMA((count,)),
+            pltpu.SemaphoreType.DMA((count,)),
         ],
         compiler_params=pltpu.CompilerParams(collective_id=2, has_side_effects=True),
         cost_estimate=pl.CostEstimate(flops=40 * 10 ** 9, bytes_accessed=8 * size * size, transcendentals=0),
@@ -430,7 +426,8 @@
     high = high_ref[...]
     low = low_ref[...]
     for index in range(4):
-        block = coeff_ref[index]
+        side, pick = divmod(index, 2)
+        block = jnp.concatenate([coeff_ref[side, piece, pick] for piece in range(coeff_ref.shape[1])], axis=0)
         final[index] = (jnp.dot(high, block, preferred_element_type=jnp.float32)
                         + jnp.dot(low, block, preferred_element_type=jnp.float32)).astype(jnp.bfloat16)
     pl.semaphore_wait(barrier, count - 1)
@@ -534,17 +531,17 @@
 
     columns = lax.dynamic_slice_in_dim(summed, half * (rank // 2), rank // 2, 1)
     gram = transposed_dot(summed, columns).reshape(tensors, rank // tensors, rank // 2)
-    coeff = jnp.stack([transposed_dot(summed, gate_rows), transposed_dot(summed, up_rows)]).astype(jnp.bfloat16)
-    coeff = coeff.reshape(2, tensors, rank // tensors, coeff.shape[2])
+    coeff = [transposed_dot(summed, rows).reshape(tensors, rank // tensors, -1) for rows in (gate_rows, up_rows)]
+    coeff = jnp.stack(coeff, axis=1).astype(jnp.bfloat16)
     gram, outgoing, coeff = lax.optimization_barrier((gram, outgoing, coeff))
     arrived = lax.all_to_all(outgoing, "expert", split_axis=0, concat_axis=0, tiled=True)
     gram, down_other = gram_sum(gram, down_weight[0])
     arrived, gram = lax.optimization_barrier((arrived, gram))
     raw = jnp.dot(arrived.reshape(experts * capacity, width), summed, preferred_element_type=jnp.float32)
-    raw = raw.astype(jnp.bfloat16).reshape(2, tensors, experts * capacity // (2 * tensors), rank)
+    raw = raw.astype(jnp.bfloat16).reshape(tensors, experts * capacity // tensors, rank)
     high, low, coeff, raw = inverse_and_sums(gram, coeff, raw)
     returned = expert_answers(
-        high, low, coeff.reshape(4, rank, -1), raw.reshape(experts * capacity, rank),
+        high, low, coeff, raw.reshape(experts * capacity, rank),
         down_weight[0], down_other, experts, capacity)
     returned = returned.reshape(experts * capacity, width)
     mixing = jnp.where(holds, shares[:, None, :], 0.0).reshape(experts * capacity, tok_rows)

time: 220 us -> 207 us (0.941)
  Pallas kernels: 191 us -> 176 us
    pallas_call x1, Pallas kernels: 68.6 us -> 51.6 us  [inverse_and_sums(): pl.pallas_call(factor_kernel, out_shape=[jax.ShapeDtypeStruct((size, size...]
  transfers between devices with their start and end apart: 1 -> 1, of which waited for: 0 -> 0; matrix products, arithmetic and copies ran while one was open for 0% -> 0% of each run, Pallas kernels for 16% -> 18%
where the time goes in v4:
time: 207 us; the launch traced here: 205 us
  Pallas kernels  176 us (85%)
  matrix products  14.9 us (7%)
  starting transfers between devices  8.28 us (4%)
  local copies, waits for them, and re-layouts  3.77 us (2%)
    pallas_call x1, Pallas kernels, inverse_and_sums(): pl.pallas_call(factor_kernel, out_shape=[jax.ShapeDtypeStruct((size, size...  51.6 us
    pallas_call x1, Pallas kernels, cluster_sum(): pl.pallas_call(cluster_kernel, out_shape=jax.ShapeDtypeStruct((rows, rank...  46.6 us
    pallas_call x1, Pallas kernels, expert_answers(): pl.pallas_call(expert_kernel, out_shape=jax.ShapeDtypeStruct((count, capa...  42.1 us
    pallas_call x1, Pallas kernels, gram_sum(): pl.pallas_call(gram_kernel, out_shape=[jax.ShapeDtypeStruct((size, size),...  35.9 us
    all_to_all x1, starting transfers between devices, on_device(): lax.all_to_all(outgoing, 'expert', split_axis=0, concat_axis=0, tiled=True)  8.28 us
    dot_general x5, matrix products, transposed_dot(): lax.dot_general(left, right, (((0,), (0,)), ((), ())), preferred_element_...  7.61 us
  transfers between devices with their start and end apart: 1, of which 0 were waited for; matrix products, arithmetic and copies ran while one was open for 0% of the time, Pallas kernels for 18%

profile of v4, /device:TPU:6, one launch (start us, length us, event | category | flops | bytes accessed | tf_op | source)
XLA Modules:
  0.0 204.7 jit_solution(14564920254341565762)
XLA Ops:
  0.0 1.2 copy-done
  1.2 1.8 fusion.7
  3.0 1.9 convolution_add_fusion.part_ref
  4.9 46.6 %shard_map.82 = bf16[896,512]{1,0:T(8,128)(2,1)} custom-call(f32[896,512]{1,0:T(8,128)} %convolution_add_fusion.part_ref, s32[32]{0:T(128)} %cluster_ref.1), custom_call_target="tpu_custom_call" | custom-call | flops 10000000000 | bytes 3670016 | tf_op jit(solution)/shard_map/pallas_call | solution.py:168
  51.5 1.5 copy.18
  53.1 0.9 copy-done.5
  54.0 0.7 fusion
  54.7 0.0 copy-start.8
  54.7 2.8 %fusion.1 = bf16[8,1,64,512]{3,2,1,0:T(8,128)(2,1)} fusion(bf16[8,64,896]{2,1,0:T(8,128)(2,1)} %bitcast.59, bf16[1,896,512]{2,1,0:T(8,128)(2,1)S(1)} %copy-done.3), kind=kOutput, calls=%fused_computation.6 | convolution fusion | flops 470024192 | bytes 2359296 | tf_op jit(solution)/shard_map/dot_general | solution.py:502
  57.5 0.1 fusion.27
  57.6 0.1 convolution_convert_fusion.4
  57.7 0.1 eq.48
  57.8 1.3 fusion.13
  59.1 0.2 fusion.17
  59.3 1.6 convolution_convert_fusion
  60.9 1.1 pad_maximum_fusion.coeff_ref
  62.0 8.3 %all-to-all-start = ((bf16[32,24,896]{2,1,0:T(8,128)(2,1)}), bf16[32,24,896]{2,1,0:T(8,128)(2,1)S(1)}, u32[]{:S(2)}, u32[]{:S(2)}) async-start(bf16[32,24,896]{2,1,0:T(8,128)(2,1)} %bitcast.9), calls=%async_computation | async-start | bytes 2752512 | tf_op jit(solution)/shard_map/all_to_all | solution.py:537
  70.3 35.9 %shard_map.83 = (f32[512,512]{1,0:T(8,128)}, bf16[512,896]{1,0:T(8,128)(2,1)}) custom-call(f32[8,64,256]{2,1,0:T(8,128)} %bitcast.67, bf16[512,896]{1,0:T(8,128)(2,1)} %bitcast.63), custom_call_target="tpu_custom_call" | custom-call | flops 40000000000 | bytes 2097152 | tf_op jit(solution)/shard_map/pallas_call | solution.py:259
  106.3 0.0 all-to-all-done
  106.3 1.9 convolution_convert_fusion.1
  108.1 51.6 %shard_map.84 = (bf16[512,512]{1,0:T(8,128)(2,1)}, bf16[512,512]{1,0:T(8,128)(2,1)}, bf16[2,8,2,64,512]{4,3,2,1,0:T(8,128)(2,1)}, bf16[8,96,512]{2,1,0:T(8,128)(2,1)}) custom-call(f32[512,512]{1,0:T(8,128)} %get-tuple-element.19.gram_ref, bf16[8,2,64,512]{3,2,1,0:T(8,128)(2,1)} %pad_maximum_fusion.coeff_ref, bf16[8,96,512]{2,1,0:T(8,128)(2,1)} %bitcast.66), custom_call_target="tpu_custom_call" | custom-call | flops 40000000000 | bytes 2097152 | tf_op jit(solution)/shard_map/pallas_call | solution.py:386
  159.8 42.1 %shard_map.85 = bf16[32,24,896]{2,1,0:T(8,128)(2,1)} custom-call(bf16[512,512]{1,0:T(8,128)(2,1)} %get-tuple-element.22.high_ref, bf16[512,512]{1,0:T(8,128)(2,1)} %get-tuple-element.23.low_ref, bf16[2,8,2,64,512]{4,3,2,1,0:T(8,128)(2,1)} %get-tuple-element.24.coeff_ref, bf16[768,512]{1,0:T(8,128)(2,1)} %bitcast.65, bf16[512,896]{1,0:T(8,128)(2,1)} %bitcast.64, ...), custom_call_target="tpu_custom_call" | custom-call | flops 20000000000 | bytes 2097152 | tf_op jit(solution)/shard_map/pallas_call | solution.py:485
  201.8 1.8 convolution_bitcast_fusion.1
  203.7 1.0 fusion.3
  (19 shorter events, 0.1 us)
Async XLA Ops:
  0.0 1.2 copy-start
  1.2 1.8 copy-start.2
  1.2 1.8 copy-start.3
  53.0 0.9 copy-start.5
  54.7 2.8 %copy-start.8 = (s32[64,8]{0,1:T(8,128)S(1)}, s32[64,8]{0,1:T(8,128)}, u32[]{:S(2)}) copy-start(s32[64,8]{0,1:T(8,128)} %param.14) | copy-start | bytes 6148
  54.7 3.1 %copy-start.4 = (bf16[896,512]{1,0:T(8,128)(2,1)S(1)}, bf16[896,512]{1,0:T(8,128)(2,1)}, u32[]{:S(2)}) copy-start(bf16[896,512]{1,0:T(8,128)(2,1)} %shard_map.82) | copy-start | bytes 2752516
  57.5 1.8 copy-start.7
  57.8 3.1 %copy-start.6 = (bf16[8,1,64,512]{3,2,1,0:T(8,128)(2,1)S(1)}, bf16[8,1,64,512]{3,2,1,0:T(8,128)(2,1)}, u32[]{:S(2)}) copy-start(bf16[8,1,64,512]{3,2,1,0:T(8,128)(2,1)} %fusion.1) | copy-start | bytes 1572868
  62.0 8.3 %copy-start.9 = (f32[64,8]{0,1:T(8,128)S(1)}, f32[64,8]{0,1:T(8,128)}, u32[]{:S(2)}) copy-start(f32[64,8]{0,1:T(8,128)} %param.15) | copy-start | bytes 6148
  62.0 44.3 %all-to-all-start = ((bf16[32,24,896]{2,1,0:T(8,128)(2,1)}), bf16[32,24,896]{2,1,0:T(8,128)(2,1)S(1)}, u32[]{:S(2)}, u32[]{:S(2)}) async-start(bf16[32,24,896]{2,1,0:T(8,128)(2,1)} %bitcast.9), calls=%async_computation | async-start | bytes 2752512 | tf_op jit(solution)/shard_map/all_to_all | solution.py:537
  201.8 1.8 copy-start.1

commit v5 on v4

--- a/solution.py
+++ b/solution.py
@@ -191,9 +191,13 @@
     )(sketched, clusters)
 
 
-def gram_kernel(part_ref, down_ref, out_ref, other_ref, arrive, pieces, rs_send, rs_recv, ag_send, ag_recv, sib_send, sib_recv, down_send, down_recv):
+def gram_kernel(part_ref, down_ref, send_ref, sum_ref, gate_ref, up_ref, out_ref, other_ref, coeff_ref, raw_ref,
+                arrive, pieces, landed, rs_send, rs_recv, ag_send, ag_recv, sib_send, sib_recv, down_send, down_recv,
+                tok_send, tok_recv):
     me = lax.axis_index("tensor")
     half = lax.axis_index("dp")
+    expert = lax.axis_index("expert")
+    experts = send_ref.shape[0]
     count = part_ref.shape[0]
     height, width = part_ref.shape[1:]
     sibling = {"dp": 1 - half}
@@ -201,7 +205,13 @@
     for step in range(1, count):
         pl.semaphore_signal(barrier, inc=1, device_id={"tensor": lax.rem(me + step, count)}, device_id_type=MESH)
     pl.semaphore_signal(barrier, inc=1, device_id=sibling, device_id_type=MESH)
-    pl.semaphore_wait(barrier, count)
+
+    def greet(step, carry):
+        pl.semaphore_signal(barrier, inc=1, device_id={"expert": lax.rem(expert + step, experts)}, device_id_type=MESH)
+        return carry
+
+    lax.fori_loop(1, experts, greet, 0)
+    pl.semaphore_wait(barrier, count + experts - 1)
 
     def scatter(step):
         peer = lax.rem(me + step, count)
@@ -221,6 +231,17 @@
         return pltpu.make_async_remote_copy(
             src_ref=pieces.at[piece], dst_ref=pieces.at[piece], send_sem=sib_send.at[step], recv_sem=sib_recv.at[step],
             device_id=sibling, device_id_type=MESH)
+
+    def route(step):
+        peer = lax.rem(expert + step, experts)
+        return pltpu.make_async_remote_copy(
+            src_ref=send_ref.at[peer], dst_ref=landed.at[expert], send_sem=tok_send.at[peer], recv_sem=tok_recv.at[expert],
+            device_id={"expert": peer}, device_id_type=MESH)
+
+    def landing(source):
+        return pltpu.make_async_remote_copy(
+            src_ref=send_ref.at[source], dst_ref=landed.at[source], send_sem=tok_send.at[source],
+            recv_sem=tok_recv.at[source], device_id={"expert": source}, device_id_type=MESH)
 
     down = pltpu.make_async_remote_copy(
         src_ref=down_ref, dst_ref=other_ref, send_sem=down_send, recv_sem=down_recv,
@@ -228,7 +249,21 @@
     order = [4, 3, 5, 2, 6, 1, 7]
     for step in order:
         scatter(step).start()
+
+    def route_all(step, carry):
+        route(step).start()
+        return carry
+
+    lax.fori_loop(1, experts, route_all, 0)
     down.start()
+    landed[expert] = send_ref[expert]
+    turned = (((0,), (0,)), ((), ()))
+    block = lax.dot_general(sum_ref[...], gate_ref[...], turned, preferred_element_type=jnp.float32)
+    for piece in range(count):
+        coeff_ref[piece, 0] = block[piece * height:(piece + 1) * height].astype(jnp.bfloat16)
+    block = lax.dot_general(sum_ref[...], up_ref[...], turned, preferred_element_type=jnp.float32)
+    for piece in range(count):
+        coeff_ref[piece, 1] = block[piece * height:(piece + 1) * height].astype(jnp.bfloat16)
     total = part_ref[me]
     for step in reversed(order):
         scatter(step).wait_recv()
@@ -252,22 +287,48 @@
         hand(step).wait_send()
     down.wait()
 
-
-def gram_sum(part, down):
+    def settle(step, carry):
+        landing(lax.rem(expert + step, experts)).wait_recv()
+        route(step).wait_send()
+        return carry
+
+    lax.fori_loop(1, experts, settle, 0)
+    capacity = send_ref.shape[1]
+    group = raw_ref.shape[1] // capacity
+
+    def project(index, carry):
+        rows = jnp.concatenate([landed[index * group + item].astype(jnp.float32) for item in range(group)], axis=0)
+        raw_ref[index] = jnp.dot(
+            rows.astype(jnp.bfloat16), sum_ref[...], preferred_element_type=jnp.float32).astype(jnp.bfloat16)
+        return carry
+
+    lax.fori_loop(0, experts // group, project, 0)
+
+
+def gram_sum(part, down, outgoing, summed, gate, up):
     count, height, width = part.shape
     size = count * height
+    experts, capacity, depth = outgoing.shape
+    vmem, any_space = pl.BlockSpec(memory_space=pltpu.VMEM), pl.BlockSpec(memory_space=pl.ANY)
     return pl.pallas_call(
         gram_kernel,
-        out_shape=[jax.ShapeDtypeStruct((size, size), jnp.float32), jax.ShapeDtypeStruct(down.shape, down.dtype)],
-        in_specs=[pl.BlockSpec(memory_space=pltpu.VMEM), pl.BlockSpec(memory_space=pl.ANY)],
-        out_specs=[pl.BlockSpec(memory_space=pltpu.VMEM), pl.BlockSpec(memory_space=pl.ANY)],
+        out_shape=[
+            jax.ShapeDtypeStruct((size, size), jnp.float32),
+            jax.ShapeDtypeStruct(down.shape, down.dtype),
+            jax.ShapeDtypeStruct((count, 2, height, gate.shape[1]), jnp.bfloat16),
+            jax.ShapeDtypeStruct((count, experts * capacity // count, size), jnp.bfloat16),
+        ],
+        in_specs=[vmem, any_space, vmem, vmem, vmem, vmem],
+        out_specs=[vmem, any_space, vmem, vmem],
         scratch_shapes=[
             pltpu.VMEM((count, height, width), jnp.float32),
             pltpu.VMEM((2 * count, height, width), jnp.float32),
-        ] + [pltpu.SemaphoreType.DMA((count,))] * 6 + [pltpu.SemaphoreType.DMA] * 2,
+            pltpu.VMEM((experts, capacity, depth), jnp.bfloat16),
+        ] + [pltpu.SemaphoreType.DMA((count,))] * 6 + [pltpu.SemaphoreType.DMA] * 2
+        + [pltpu.SemaphoreType.DMA((experts,))] * 2,
         compiler_params=pltpu.CompilerParams(collective_id=1, has_side_effects=True),
         cost_estimate=pl.CostEstimate(flops=40 * 10 ** 9, bytes_accessed=8 * size * size, transcendentals=0),
-    )(part, down)
+    )(part, down, outgoing, summed, gate, up)
 
 
 def factor_kernel(gram_ref, coeff_ref, raw_ref, high_ref, low_ref, coeff_all, raw_all, out_ref, inv_ref, coeff_slot, raw_slot,
@@ -531,14 +592,7 @@
 
     columns = lax.dynamic_slice_in_dim(summed, half * (rank // 2), rank // 2, 1)
     gram = transposed_dot(summed, columns).reshape(tensors, rank // tensors, rank // 2)
-    coeff = [transposed_dot(summed, rows).reshape(tensors, rank // tensors, -1) for rows in (gate_rows, up_rows)]
-    coeff = jnp.stack(coeff, axis=1).astype(jnp.bfloat16)
-    gram, outgoing, coeff = lax.optimization_barrier((gram, outgoing, coeff))
-    arrived = lax.all_to_all(outgoing, "expert", split_axis=0, concat_axis=0, tiled=True)
-    gram, down_other = gram_sum(gram, down_weight[0])
-    arrived, gram = lax.optimization_barrier((arrived, gram))
-    raw = jnp.dot(arrived.reshape(experts * capacity, width), summed, preferred_element_type=jnp.float32)
-    raw = raw.astype(jnp.bfloat16).reshape(tensors, experts * capacity // tensors, rank)
+    gram, down_other, coeff, raw = gram_sum(gram, down_weight[0], outgoing, summed, gate_rows, up_rows)
     high, low, coeff, raw = inverse_and_sums(gram, coeff, raw)
     returned = expert_answers(
         high, low, coeff, raw.reshape(experts * capacity, rank),

time: 207 us -> 204 us (0.986)
  Pallas kernels: 176 us -> 191 us
  starting transfers between devices: 8.28 us -> 0 us
  matrix products: 14.9 us -> 10.9 us
  local copies, waits for them, and re-layouts: 3.77 us -> 0.12 us
    pallas_call x1, Pallas kernels: 35.9 us -> 45.4 us  [gram_sum(): pl.pallas_call(gram_kernel, out_shape=[jax.ShapeDtypeStruct((size, size),...]
    all_to_all x1 -> x0, starting transfers between devices: 8.28 us -> none  [on_device(): lax.all_to_all(outgoing, 'expert', split_axis=0, concat_axis=0, tiled=True)]
    pallas_call x1, Pallas kernels: 51.6 us -> 54.9 us  [inverse_and_sums(): pl.pallas_call(factor_kernel, out_shape=[jax.ShapeDtypeStruct((size, size...]
    pallas_call x1, Pallas kernels: 42.1 us -> 44.3 us  [expert_answers(): pl.pallas_call(expert_kernel, out_shape=jax.ShapeDtypeStruct((count, capa...]
    dot_general x5 -> x3, matrix products: 7.61 us -> 5.43 us  [transposed_dot(): lax.dot_general(left, right, (((0,), (0,)), ((), ())), preferred_element_...]
    unnamed x20 -> x12, local copies, waits for them, and re-layouts: 2.15 us -> 0.03 us
  transfers between devices with their start and end apart: 1 -> 0, of which waited for: 0 -> 0; matrix products, arithmetic and copies ran while one was open for 0% -> 0% of each run, Pallas kernels for 18% -> 0%
where the time goes in v5:
time: 204 us; the launch traced here: 203 us
  Pallas kernels  191 us (94%)
  matrix products  10.9 us (5%)
    pallas_call x1, Pallas kernels, inverse_and_sums(): pl.pallas_call(factor_kernel, out_shape=[jax.ShapeDtypeStruct((size, size...  54.9 us
    pallas_call x1, Pallas kernels, cluster_sum(): pl.pallas_call(cluster_kernel, out_shape=jax.ShapeDtypeStruct((rows, rank...  46.6 us
    pallas_call x1, Pallas kernels, gram_sum(): pl.pallas_call(gram_kernel, out_shape=[jax.ShapeDtypeStruct((size, size),...  45.4 us
    pallas_call x1, Pallas kernels, expert_answers(): pl.pallas_call(expert_kernel, out_shape=jax.ShapeDtypeStruct((count, capa...  44.3 us
    dot_general x3, matrix products, transposed_dot(): lax.dot_general(left, right, (((0,), (0,)), ((), ())), preferred_element_...  5.43 us

profile of v5, /device:TPU:6, one launch (start us, length us, event | category | flops | bytes accessed | tf_op | source)
XLA Modules:
  0.0 203.4 jit_solution(8768459492263964502)
XLA Ops:
  0.0 0.0 copy-start
  0.0 0.8 fusion.21
  0.8 0.1 convolution_convert_fusion.1
  1.0 0.1 eq.48
  1.1 0.2 fusion.11
  1.2 0.0 copy-done
  1.3 1.6 convolution_convert_fusion
  2.9 0.0 copy-done.2
  2.9 1.9 fusion.3
  4.8 0.0 copy-done.3
  4.8 1.9 convolution_add_fusion.part_ref
  6.7 46.6 %shard_map.82.sum_ref = bf16[896,512]{1,0:T(8,128)(2,1)} custom-call(f32[896,512]{1,0:T(8,128)} %convolution_add_fusion.part_ref, s32[32]{0:T(128)} %cluster_ref.1), custom_call_target="tpu_custom_call" | custom-call | flops 10000000000 | bytes 3670016 | tf_op jit(solution)/shard_map/pallas_call | solution.py:168
  53.3 2.6 %fusion.7 = f32[512,256]{1,0:T(8,128)} fusion(bf16[896,512]{1,0:T(8,128)(2,1)} %shard_map.82.sum_ref, s32[]{:T(128)S(6)} %select_n.16), kind=kOutput, calls=%fused_computation.14 | convolution fusion | flops 234881024 | bytes 1900548 | tf_op jit(solution)/shard_map/dot_general | solution.py:563
  55.8 45.4 %shard_map.83 = (f32[512,512]{1,0:T(8,128)}, bf16[512,896]{1,0:T(8,128)(2,1)}, bf16[8,2,64,512]{3,2,1,0:T(8,128)(2,1)}, bf16[8,96,512]{2,1,0:T(8,128)(2,1)}) custom-call(f32[8,64,256]{2,1,0:T(8,128)} %bitcast.47, bf16[512,896]{1,0:T(8,128)(2,1)} %bitcast.44, bf16[32,24,896]{2,1,0:T(8,128)(2,1)} %bitcast.38, bf16[896,512]{1,0:T(8,128)(2,1)} %shard_map.82.sum_ref, ...), custom_call_target="tpu_custom_call" | custom-call | flops 40000000000 | bytes 2097152 | tf_op jit(solution)/shard_map/pallas_call | solution.py:313
  101.2 54.9 %shard_map.84 = (bf16[512,512]{1,0:T(8,128)(2,1)}, bf16[512,512]{1,0:T(8,128)(2,1)}, bf16[2,8,2,64,512]{4,3,2,1,0:T(8,128)(2,1)}, bf16[8,96,512]{2,1,0:T(8,128)(2,1)}) custom-call(f32[512,512]{1,0:T(8,128)} %get-tuple-element.13.gram_ref, bf16[8,2,64,512]{3,2,1,0:T(8,128)(2,1)} %get-tuple-element.14.coeff_ref, bf16[8,96,512]{2,1,0:T(8,128)(2,1)} %get-tuple-element.15.raw_ref), custom_call_target="tpu_custom_call" | custom-call | flops 40000000000 | bytes 2097152 | tf_op jit(solution)/shard_map/pallas_call | solution.py:447
  156.1 0.0 copy-start.4
  156.1 0.0 copy-start.5
  156.1 44.3 %shard_map.85 = bf16[32,24,896]{2,1,0:T(8,128)(2,1)} custom-call(bf16[512,512]{1,0:T(8,128)(2,1)} %get-tuple-element.16.high_ref, bf16[512,512]{1,0:T(8,128)(2,1)} %get-tuple-element.17.low_ref, bf16[2,8,2,64,512]{4,3,2,1,0:T(8,128)(2,1)} %get-tuple-element.18.coeff_ref, bf16[768,512]{1,0:T(8,128)(2,1)} %bitcast.46, bf16[512,896]{1,0:T(8,128)(2,1)} %bitcast.45, ...), custom_call_target="tpu_custom_call" | custom-call | flops 20000000000 | bytes 2097152 | tf_op jit(solution)/shard_map/pallas_call | solution.py:546
  200.4 0.0 copy-start.1
  200.4 0.0 copy-done.4
  200.4 0.0 copy-done.5
  200.5 1.8 convolution_bitcast_fusion.1
  202.3 0.0 copy-done.1
  202.3 1.0 fusion.1
  (4 shorter events, 0.1 us)
Async XLA Ops:
  0.0 1.2 copy-start
  0.0 2.9 %copy-start.2 = (bf16[1,2,512,512]{3,2,1,0:T(8,128)(2,1)S(1)}, bf16[1,2,512,512]{3,2,1,0:T(8,128)(2,1)}, u32[]{:S(2)}) copy-start(bf16[1,2,512,512]{3,2,1,0:T(8,128)(2,1)} %param.12) | copy-start | bytes 3145732
  2.9 1.9 copy-start.3
  156.1 44.3 %copy-start.4 = (s32[64,8]{0,1:T(8,128)S(1)}, s32[64,8]{0,1:T(8,128)}, u32[]{:S(2)}) copy-start(s32[64,8]{0,1:T(8,128)} %param.14) | copy-start | bytes 6148
  156.1 44.3 %copy-start.5 = (f32[64,8]{0,1:T(8,128)S(1)}, f32[64,8]{0,1:T(8,128)}, u32[]{:S(2)}) copy-start(f32[64,8]{0,1:T(8,128)} %param.15) | copy-start | bytes 6148
  200.4 1.9 copy-start.1

commit v6 on v4

v6 whole, which is shorter than its diff:
```python
import jax
import jax.numpy as jnp
from jax import lax
from jax.experimental import pallas as pl
from jax.experimental.pallas import tpu as pltpu
from jax.sharding import PartitionSpec as P

MESH = pl.DeviceIdType.MESH
HIGHEST = lax.Precision.HIGHEST
BLK = 128


def factor_block(tiles, serve):
    lane = lax.broadcasted_iota(jnp.int32, (8, BLK), 1)
    sub = lax.broadcasted_iota(jnp.int32, (8, BLK), 0)
    n = BLK // 8
    tiles = list(tiles)
    for k in range(0, BLK, 2):
        t, r = divmod(k, 8)
        cur = tiles[t]
        col1 = jnp.broadcast_to(cur[:, k:k + 1], (8, BLK))
        col2 = jnp.broadcast_to(cur[:, k + 1:k + 2], (8, BLK))
        a = col1[r:r + 1, :]
        b = col1[r + 1:r + 2, :]
        c = col2[r + 1:r + 2, :]
        ra = 1.0 / a
        rc = a / (a * c - b * b)
        first, second = lane == k, lane == k + 1
        both = jnp.logical_or(first, second)
        row1 = jnp.where(first[:1], 1.0, jnp.where(second[:1], 0.0, cur[r:r + 1, :]))
        row2 = jnp.where(both[:1], 0.0, cur[r + 1:r + 2, :]) - (b * ra) * row1
        row2 = jnp.where(second[:1], 1.0, row2)
        v2 = rc * row2
        v1 = ra * row1 - (b * ra) * v2
        for i in range(t, n):
            old = tiles[i]
            if i == t:
                new = jnp.where(both, 0.0, old) - col1 * v1 - col2 * v2
                new = jnp.where(sub > r + 1, new, old)
                new = jnp.where(sub == r, row1 * jnp.sqrt(ra), new)
                new = jnp.where(sub == r + 1, row2 * jnp.sqrt(rc), new)
            else:
                c1 = jnp.broadcast_to(old[:, k:k + 1], (8, BLK))
                c2 = jnp.broadcast_to(old[:, k + 1:k + 2], (8, BLK))
                new = jnp.where(both, 0.0, old) - c1 * v1 - c2 * v2
            tiles[i] = new
        if k % 32 == 30:
            serve(k // 32)
    return [jnp.where(lane <= sub + 8 * i, tiles[i], 0.0) for i in range(n)]

def eliminate(out_ref, inv_ref, serve):
    size = out_ref.shape[0]
    steps = size // BLK

    def step(j, carry):
        at = pl.multiple_of(j * BLK, BLK)
        tiles = [out_ref[pl.ds(pl.multiple_of(at + 8 * i, 8), 8), pl.ds(at, BLK)] for i in range(BLK // 8)]
        for i, tile in enumerate(factor_block(tiles, lambda turn: serve(turn % 2, 2 * j + turn // 2))):
            inv_ref[8 * i:8 * i + 8, :] = tile
        inv = inv_ref[...]
        rows = lax.broadcasted_iota(jnp.int32, (BLK, BLK), 0)
        cols = lax.broadcasted_iota(jnp.int32, (BLK, BLK), 1)
        eye = jnp.where(rows == cols, 1.0, 0.0)
        out_ref[pl.ds(at, BLK), pl.ds(at, BLK)] = eye
        full = jnp.dot(inv, out_ref[pl.ds(at, BLK), :], precision=HIGHEST, preferred_element_type=jnp.float32)
        column = lax.broadcasted_iota(jnp.int32, (BLK, size), 1)
        later = jnp.where(column >= at + BLK, full, 0.0)
        out_ref[pl.ds(at, BLK), :] = full
        column = lax.broadcasted_iota(jnp.int32, (size, size), 1)
        row = lax.broadcasted_iota(jnp.int32, (size, size), 0)
        zero = (column >= at) & (column < at + BLK) & (row >= at + BLK)
        out_ref[...] = jnp.where(zero, 0.0, out_ref[...]) - lax.dot_general(
            later, full, (((0,), (0,)), ((), ())), precision=HIGHEST, preferred_element_type=jnp.float32)
        return carry

    lax.fori_loop(0, steps, step, 0)
    row = lax.broadcasted_iota(jnp.int32, (size, size), 0)
    column = lax.broadcasted_iota(jnp.int32, (size, size), 1)
    out_ref[...] = jnp.where(column <= row, out_ref[...], 0.0)

REACH = 3
CUTS = 7


def cluster_kernel(part_ref, cluster_ref, out_ref, stage, got, own, plus, minus, acc,
                   dp_send, dp_recv, up_send, up_recv, low_send, low_recv, fin_send, fin_recv):
    count = lax.axis_size("expert")
    me = lax.axis_index("expert")
    half = lax.axis_index("dp")
    sibling = {"dp": 1 - half}
    after = {"expert": lax.rem(me + 1, count)}
    before = {"expert": lax.rem(me + count - 1, count)}
    part = part_ref.shape[0] // 2
    size = part // CUTS
    mine = cluster_ref[me]

    def share(step):
        other = me + step
        inside = jnp.logical_and(other >= 0, other < count)
        same = cluster_ref[lax.rem(other + count, count)] == mine
        return jnp.where(jnp.logical_and(inside, same), 1.0, 0.0).astype(jnp.float32)

    barrier = pltpu.get_barrier_semaphore()
    for device in (sibling, after, before):
        pl.semaphore_signal(barrier, inc=1, device_id=device, device_id_type=MESH)

    def rows(side, cut):
        return pl.ds(pl.multiple_of(side * part + cut * size, 16), size)

    def remote(src, dst, send, recv, device):
        return pltpu.make_async_remote_copy(
            src_ref=src, dst_ref=dst, send_sem=send, recv_sem=recv, device_id=device, device_id_type=MESH)

    def swap(cut):
        return remote(stage.at[cut], got.at[cut], dp_send.at[cut], dp_recv.at[cut], sibling)

    def ahead(hop, cut):
        source = own.at[cut] if hop == 0 else plus.at[hop - 1, cut]
        return remote(source, plus.at[hop, cut], up_send.at[hop, cut], up_recv.at[hop, cut], after)

    def back(hop, cut):
        source = own.at[cut] if hop == 0 else minus.at[hop - 1, cut]
        return remote(source, minus.at[hop, cut], low_send.at[hop, cut], low_recv.at[hop, cut], before)

    def finish(cut):
        place = out_ref.at[rows(half, cut)]
        return remote(place, place, fin_send.at[cut], fin_recv.at[cut], sibling)

    for cut in range(CUTS):
        stage[cut] = part_ref[rows(1 - half, cut), :].astype(jnp.bfloat16)
    pl.semaphore_wait(barrier, 3)
    for cut in range(CUTS):
        swap(cut).start()
    for cut in range(CUTS):
        swap(cut).wait_recv()
        value = (part_ref[rows(half, cut), :] + got[cut].astype(jnp.float32)).astype(jnp.bfloat16)
        own[cut] = value
        ahead(0, cut).start()
        back(0, cut).start()
        acc[cut] = value.astype(jnp.float32)
    for hop in range(REACH):
        for cut in range(CUTS):
            ahead(hop, cut).wait_recv()
            if hop < REACH - 1:
                ahead(hop + 1, cut).start()
            back(hop, cut).wait_recv()
            if hop < REACH - 1:
                back(hop + 1, cut).start()
            total = acc[cut] + share(-1 - hop) * plus[hop, cut].astype(jnp.float32)
            total = total + share(hop + 1) * minus[hop, cut].astype(jnp.float32)
            if hop < REACH - 1:
                acc[cut] = total
            else:
                out_ref[rows(half, cut), :] = total.astype(jnp.bfloat16)
                finish(cut).start()
    for cut in range(CUTS):
        finish(cut).wait_recv()
        finish(cut).wait_send()
        swap(cut).wait_send()
        for hop in range(REACH):
            ahead(hop, cut).wait_send()
            back(hop, cut).wait_send()


def cluster_sum(sketched, clusters):
    rows, rank = sketched.shape
    size = rows // 2 // CUTS
    return pl.pallas_call(
        cluster_kernel,
        out_shape=jax.ShapeDtypeStruct((rows, rank), jnp.bfloat16),
        in_specs=[pl.BlockSpec(memory_space=pltpu.VMEM), pl.BlockSpec(memory_space=pltpu.SMEM)],
        out_specs=pl.BlockSpec(memory_space=pltpu.VMEM),
        scratch_shapes=[
            pltpu.VMEM((CUTS, size, rank), jnp.bfloat16),
            pltpu.VMEM((CUTS, size, rank), jnp.bfloat16),
            pltpu.VMEM((CUTS, size, rank), jnp.bfloat16),
            pltpu.VMEM((REACH, CUTS, size, rank), jnp.bfloat16),
            pltpu.VMEM((REACH, CUTS, size, rank), jnp.bfloat16),
            pltpu.VMEM((CUTS, size, rank), jnp.float32),
            pltpu.SemaphoreType.DMA((CUTS,)),
            pltpu.SemaphoreType.DMA((CUTS,)),
            pltpu.SemaphoreType.DMA((REACH, CUTS)),
            pltpu.SemaphoreType.DMA((REACH, CUTS)),
            pltpu.SemaphoreType.DMA((REACH, CUTS)),
            pltpu.SemaphoreType.DMA((REACH, CUTS)),
            pltpu.SemaphoreType.DMA((CUTS,)),
            pltpu.SemaphoreType.DMA((CUTS,)),
        ],
        compiler_params=pltpu.CompilerParams(collective_id=3, has_side_effects=True),
        cost_estimate=pl.CostEstimate(flops=10 ** 10, bytes_accessed=8 * rows * rank, transcendentals=0),
    )(sketched, clusters)


GROUP = 8


def whole_kernel(part_ref, down_ref, send_ref, sum_ref, gate_ref, up_ref, back_ref,
                 arrive, pieces, landed, other, coeff_part, raw_part, work, inv_ref, coeff_slot, raw_slot,
                 high_ref, low_ref, coeff_all, raw_all, final, answers,
                 rs_send, rs_recv, ag_send, ag_recv, hand_send, hand_recv, down_send, down_recv, tok_send, tok_recv,
                 ring_send, ring_recv, share_send, share_recv, ans_send, ans_recv):
    me = lax.axis_index("tensor")
    half = lax.axis_index("dp")
    expert = lax.axis_index("expert")
    experts, capacity, depth = send_ref.shape
    count, height, width = part_ref.shape
    longer = count // 2
    reach = (longer, longer - 1)
    sibling = {"dp": 1 - half}
    after = {"tensor": lax.rem(me + 1, count)}
    before = {"tensor": lax.rem(me + count - 1, count)}
    parts, slots = (coeff_part, raw_part), (coeff_slot, raw_slot)
    barrier = pltpu.get_barrier_semaphore()
    for step in range(1, count):
        pl.semaphore_signal(barrier, inc=1, device_id={"tensor": lax.rem(me + step, count)}, device_id_type=MESH)
    pl.semaphore_signal(barrier, inc=1, device_id=sibling, device_id_type=MESH)

    def greet(step, carry):
        pl.semaphore_signal(barrier, inc=1, device_id={"expert": lax.rem(expert + step, experts)}, device_id_type=MESH)
        return carry

    lax.fori_loop(1, experts, greet, 0)
    pl.semaphore_wait(barrier, count + experts - 1)

    def remote(src, dst, send, recv, device):
        return pltpu.make_async_remote_copy(
            src_ref=src, dst_ref=dst, send_sem=send, recv_sem=recv, device_id=device, device_id_type=MESH)

    def scatter(step):
        peer = lax.rem(me + step, count)
        return remote(part_ref.at[peer], arrive.at[step], rs_send.at[step], rs_recv.at[step], {"tensor": peer})

    def spread(step):
        mine = pieces.at[half * count + me]
        return remote(mine, mine, ag_send.at[step], ag_recv.at[step], {"tensor": lax.rem(me + step, count)})

    def hand(step):
        piece = pieces.at[half * count + lax.rem(me + count - step, count)]
        return remote(piece, piece, hand_send.at[step], hand_recv.at[step], sibling)

    def route(step):
        peer = lax.rem(expert + step, experts)
        return remote(send_ref.at[peer], landed.at[expert], tok_send.at[peer], tok_recv.at[expert], {"expert": peer})

    def landing(source):
        return remote(send_ref.at[source], landed.at[source], tok_send.at[source], tok_recv.at[source], {"expert": source})

    def upward(kind, side):
        return kind == side

    def chunk(kind, side, distance):
        return lax.rem(me + (distance if upward(kind, side) else count - distance), count)

    def place(kind, index):
        return coeff_all.at[0, index] if kind == 0 else raw_all.at[index]

    def ring(src, dst, kind, side, turn):
        return remote(src, dst, ring_send.at[kind, side, turn], ring_recv.at[kind, side, turn],
                      after if upward(kind, side) else before)

    def first(kind, side):
        return ring(parts[kind].at[chunk(kind, side, reach[side])], slots[kind].at[side, 0], kind, side, 0)

    def add_on(kind, side, turn):
        return ring(slots[kind].at[side, turn - 1], slots[kind].at[side, turn], kind, side, turn)

    def pass_on(kind, side, hop):
        here = place(kind, lax.rem(me + (count - hop if upward(kind, side) else hop), count))
        return ring(here, here, kind, side, longer + hop)

    def share(index):
        return remote(coeff_all.at[0, index], coeff_all.at[1, index], share_send.at[index], share_recv.at[index], sibling)

    def serve(kind, turn):
        for side in range(2):
            @pl.when(turn < reach[side])
            def _():
                slot = slots[kind].at[side, turn]
                ring(slot, slot, kind, side, turn).wait_recv()

            @pl.when(turn < reach[side] - 1)
            def _():
                value = parts[kind][chunk(kind, side, reach[side] - 1 - turn)].astype(jnp.float32)
                slots[kind][side, turn] = (slots[kind][side, turn].astype(jnp.float32) + value).astype(jnp.bfloat16)
                add_on(kind, side, turn + 1).start()

        @pl.when(turn == longer - 1)
        def _():
            value = parts[kind][me].astype(jnp.float32) + slots[kind][0, longer - 1].astype(jnp.float32)
            value = value + slots[kind][1, longer - 2].astype(jnp.float32)
            place(kind, me)[...] = value.astype(jnp.bfloat16)
            for side in range(2):
                pass_on(kind, side, 0).start()
            if kind == 0:
                share(me).start()

        hop = turn - longer
        for side in range(2):
            index = lax.rem(me + (2 * count - 1 - hop if upward(kind, side) else hop + 1), count)

            @pl.when((hop >= 0) & (hop < reach[side]))
            def _():
                ring(place(kind, index), place(kind, index), kind, side, turn).wait_recv()
                if kind == 0:
                    share(index).start()

            @pl.when((hop >= 0) & (hop < reach[side] - 1))
            def _():
                pass_on(kind, side, hop + 1).start()

    down = remote(down_ref, other, down_send, down_recv, sibling)
    order = [4, 3, 5, 2, 6, 1, 7]
    for step in order:
        scatter(step).start()

    def route_all(step, carry):
        route(step).start()
        return carry

    lax.fori_loop(1, experts, route_all, 0)
    down.start()
    landed[expert] = send_ref[expert]
    turned = (((0,), (0,)), ((), ()))
    for pick, rows_ref in enumerate((gate_ref, up_ref)):
        block = lax.dot_general(sum_ref[...], rows_ref[...], turned, preferred_element_type=jnp.float32)
        for piece in range(count):
            coeff_part[piece, pick] = block[piece * height:(piece + 1) * height].astype(jnp.bfloat16)
    total = part_ref[me]
    for step in reversed(order):
        scatter(step).wait_recv()
        total = total + arrive[step]
    pieces[half * count + me] = total
    for step in order:
        spread(step).start()
    hand(0).start()
    for side in range(2):
        first(0, side).start()
    for step in reversed(order):
        spread(step).wait_recv()
        hand(step).start()
    for step in range(count):
        hand(step).wait_recv()
    for side in range(2):
        for piece in range(count):
            work[piece * height:(piece + 1) * height, side * width:(side + 1) * width] = pieces[side * count + piece]

    def settle(step, carry):
        landing(lax.rem(expert + step, experts)).wait_recv()
        return carry

    lax.fori_loop(1, experts, settle, 0)
    group = raw_part.shape[1] // capacity

    def project(index, carry):
        rows = jnp.concatenate([landed[index * group + item].astype(jnp.float32) for item in range(group)], axis=0)
        raw_part[index] = jnp.dot(
            rows.astype(jnp.bfloat16), sum_ref[...], preferred_element_type=jnp.float32).astype(jnp.bfloat16)
        return carry

    lax.fori_loop(0, experts // group, project, 0)
    for side in range(2):
        first(1, side).start()
    eliminate(work, inv_ref, serve)
    high = work[...].astype(jnp.bfloat16)
    high_ref[...] = high
    low_ref[...] = (work[...] - high.astype(jnp.float32)).astype(jnp.bfloat16)

    def gathered(index, carry):
        share(index).wait_recv()
        return carry

    lax.fori_loop(0, count, gathered, 0)
    down.wait_recv()
    low = low_ref[...]
    for index in range(4):
        side, pick = divmod(index, 2)
        block = jnp.concatenate([coeff_all[side, piece, pick] for piece in range(count)], axis=0)
        final[index] = (jnp.dot(high, block, preferred_element_type=jnp.float32)
                        + jnp.dot(low, block, preferred_element_type=jnp.float32)).astype(jnp.bfloat16)

    def give(target):
        return remote(answers.at[target], back_ref.at[expert], ans_send.at[target], ans_recv.at[expert], {"expert": target})

    def take(source):
        return remote(back_ref.at[source], back_ref.at[source], ans_send.at[source], ans_recv.at[source], {"expert": source})

    dims = (((1,), (1,)), ((), ()))
    groups = experts // GROUP
    span = GROUP * capacity
    each = span // raw_all.shape[1]

    def compute(turn, carry):
        block = lax.rem(expert // GROUP + turn, groups)
        rows = jnp.concatenate([raw_all[block * each + item] for item in range(each)], axis=0)
        projected = (lax.dot_general(rows, high_ref[...], dims, preferred_element_type=jnp.float32)
                     + lax.dot_general(rows, low_ref[...], dims, preferred_element_type=jnp.float32)).astype(jnp.bfloat16)
        result = jnp.zeros((span, depth), jnp.float32)
        for side, rows_ref in enumerate((down_ref, other)):
            gate = jnp.dot(projected, final[2 * side], preferred_element_type=jnp.float32)
            up = jnp.dot(projected, final[2 * side + 1], preferred_element_type=jnp.float32)
            hidden = (gate / (1.0 + jnp.exp(-gate)) * up).astype(jnp.bfloat16)
            result = result + jnp.dot(hidden, rows_ref[...], preferred_element_type=jnp.float32)
        for index in range(GROUP):
            target = block * GROUP + index
            value = result[index * capacity:(index + 1) * capacity].astype(jnp.bfloat16)

            @pl.when(target == expert)
            def _():
                back_ref[expert] = value

            @pl.when(target != expert)
            def _():
                answers[target] = value
                give(target).start()
        return carry

    lax.fori_loop(0, groups, compute, 0)
    for step in order:
        scatter(step).wait_send()
        spread(step).wait_send()
    for step in range(count):
        hand(step).wait_send()
        share(step).wait_send()
    down.wait_send()
    for kind in range(2):
        for side in range(2):
            first(kind, side).wait_send()
            for turn in range(1, reach[side]):
                add_on(kind, side, turn).wait_send()
            for hop in range(reach[side]):
                pass_on(kind, side, hop).wait_send()

    def drain(step, carry):
        route(step).wait_send()
        take(lax.rem(expert + step, experts)).wait_recv()
        give(lax.rem(expert + step, experts)).wait_send()
        return carry

    lax.fori_loop(1, experts, drain, 0)


def expert_answers(part, down, outgoing, summed, gate, up):
    count, height, width = part.shape
    size = count * height
    experts, capacity, depth = outgoing.shape
    hidden = gate.shape[1]
    rows = experts * capacity // count
    low, full = jnp.bfloat16, jnp.float32
    dma = pltpu.SemaphoreType.DMA
    return pl.pallas_call(
        whole_kernel,
        out_shape=jax.ShapeDtypeStruct(outgoing.shape, low),
        in_specs=[pl.BlockSpec(memory_space=pltpu.VMEM)] * 6,
        out_specs=pl.BlockSpec(memory_space=pltpu.VMEM),
        scratch_shapes=[
            pltpu.VMEM((count, height, width), full),
            pltpu.VMEM((2 * count, height, width), full),
            pltpu.VMEM((experts, capacity, depth), low),
            pltpu.VMEM(down.shape, low),
            pltpu.VMEM((count, 2, height, hidden), low),
            pltpu.VMEM((count, rows, size), low),
            pltpu.VMEM((size, size), full),
            pltpu.VMEM((BLK, BLK), full),
            pltpu.VMEM((2, count // 2, 2, height, hidden), low),
            pltpu.VMEM((2, count // 2, rows, size), low),
            pltpu.VMEM((size, size), low),
            pltpu.VMEM((size, size), low),
            pltpu.VMEM((2, count, 2, height, hidden), low),
            pltpu.VMEM((count, rows, size), low),
            pltpu.VMEM((4, size, hidden), low),
            pltpu.VMEM((experts, capacity, depth), low),
        ] + [dma((count,))] * 6 + [dma] * 2 + [dma((experts,))] * 2 + [dma((2, 2, count))] * 2 + [dma((count,))] * 2
        + [dma((experts,))] * 2,
        compiler_params=pltpu.CompilerParams(collective_id=1, has_side_effects=True),
        cost_estimate=pl.CostEstimate(flops=10 ** 11, bytes_accessed=8 * size * size, transcendentals=0),
    )(part, down, outgoing, summed, gate, up)


def transposed_dot(left, right):
    return lax.dot_general(left, right, (((0,), (0,)), ((), ())), preferred_element_type=jnp.float32)


def on_device(tokens, gate_weight, up_weight, down_weight, sketch, clusters, routes, route_weights):
    gate_rows = gate_weight[0]
    up_rows = up_weight[0]
    experts = lax.axis_size("expert")
    tensors = lax.axis_size("tensor")
    half = lax.axis_index("dp")
    sketched = jnp.dot(gate_rows, sketch[0, 0], preferred_element_type=jnp.float32) + jnp.dot(
        up_rows, sketch[0, 1], preferred_element_type=jnp.float32
    )
    rank = sketched.shape[1]

    summed = cluster_sum(sketched, clusters)

    tok_rows, width = tokens.shape
    top_count = routes.shape[1]
    capacity = tok_rows * top_count * 3 // (2 * experts)
    named = routes.T[None] == jnp.arange(experts, dtype=jnp.int32)[:, None, None]
    chosen = jnp.any(named, axis=1)
    shares = jnp.sum(jnp.where(named, route_weights.T[None], 0.0), axis=1)
    token_index = jnp.arange(tok_rows)
    earlier = (token_index[:, None] < token_index[None, :]).astype(jnp.bfloat16)
    place = jnp.dot(chosen.astype(jnp.bfloat16), earlier, preferred_element_type=jnp.float32).astype(jnp.int32)
    holds = chosen[:, None, :] & (place[:, None, :] == jnp.arange(capacity, dtype=jnp.int32)[None, :, None])
    select = holds.astype(jnp.bfloat16).reshape(experts * capacity, tok_rows)
    outgoing = jnp.dot(select, tokens, preferred_element_type=jnp.float32).astype(jnp.bfloat16)
    outgoing = outgoing.reshape(experts, capacity, width)

    columns = lax.dynamic_slice_in_dim(summed, half * (rank // 2), rank // 2, 1)
    gram = transposed_dot(summed, columns).reshape(tensors, rank // tensors, rank // 2)
    returned = expert_answers(gram, down_weight[0], outgoing, summed, gate_rows, up_rows)
    returned = returned.reshape(experts * capacity, width)
    mixing = jnp.where(holds, shares[:, None, :], 0.0).reshape(experts * capacity, tok_rows)
    high = mixing.astype(jnp.bfloat16)
    low = (mixing - high.astype(jnp.float32)).astype(jnp.bfloat16)
    return (transposed_dot(high, returned) + transposed_dot(low, returned)).astype(jnp.bfloat16)


def solution(mesh):
    return jax.shard_map(
        on_device,
        mesh=mesh,
        in_specs=(
            P(("expert", "dp"), "tensor"),
            P("expert", "tensor", "dp"),
            P("expert", "tensor", "dp"),
            P("expert", "dp", "tensor"),
            P("expert", None, "dp", None),
            P(),
            P(("expert", "dp"), None),
            P(("expert", "dp"), None),
        ),
        out_specs=P(("expert", "dp"), "tensor"),
        check_vma=False,
    )
```

time: 207 us -> 187 us (0.903)
  starting transfers between devices: 8.28 us -> 0 us
  matrix products: 14.9 us -> 10.9 us
  local copies, waits for them, and re-layouts: 3.77 us -> 0.11 us
    all_to_all x1 -> x0, starting transfers between devices: 8.28 us -> none  [on_device(): lax.all_to_all(outgoing, 'expert', split_axis=0, concat_axis=0, tiled=True)]
    pallas_call x3 -> x1, Pallas kernels: 130 us -> 127 us  [expert_answers(): pl.pallas_call(whole_kernel, out_shape=jax.ShapeDtypeStruct(outgoing.shap...]
    dot_general x5 -> x3, matrix products: 7.61 us -> 5.43 us  [transposed_dot(): lax.dot_general(left, right, (((0,), (0,)), ((), ())), preferred_element_...]
    unnamed x20 -> x12, local copies, waits for them, and re-layouts: 2.15 us -> 0.02 us
  transfers between devices with their start and end apart: 1 -> 0, of which waited for: 0 -> 0; matrix products, arithmetic and copies ran while one was open for 0% -> 0% of each run, Pallas kernels for 18% -> 0%
where the time goes in v6:
time: 187 us; the launch traced here: 186 us
  Pallas kernels  174 us (93%)
  matrix products  10.9 us (6%)
    pallas_call x1, Pallas kernels, expert_answers(): pl.pallas_call(whole_kernel, out_shape=jax.ShapeDtypeStruct(outgoing.shap...  127 us
    pallas_call x1, Pallas kernels, cluster_sum(): pl.pallas_call(cluster_kernel, out_shape=jax.ShapeDtypeStruct((rows, rank...  46.6 us
    dot_general x3, matrix products, transposed_dot(): lax.dot_general(left, right, (((0,), (0,)), ((), ())), preferred_element_...  5.43 us

profile of v6, /device:TPU:6, one launch (start us, length us, event | category | flops | bytes accessed | tf_op | source)
XLA Modules:
  0.0 185.9 jit_solution(13352083943807119418)
XLA Ops:
  0.0 0.0 copy-start
  0.0 0.0 copy-start.2
  0.0 0.8 fusion.21
  0.8 0.1 convolution_convert_fusion.1
  1.0 0.1 eq.48
  1.1 0.2 fusion.11
  1.2 0.0 copy-done
  1.3 1.6 convolution_convert_fusion
  2.9 0.0 copy-done.2
  2.9 0.0 copy-start.3
  2.9 1.9 %fusion.3 = f32[896,512]{1,0:T(8,128)S(1)} fusion(bf16[1,2,512,512]{3,2,1,0:T(8,128)(2,1)S(1)} %copy-done.2, bf16[1,896,512]{2,1,0:T(8,128)(2,1)} %param.9), kind=kOutput, calls=%fused_computation.8 | convolution fusion | flops 469762048 | bytes 3276800 | tf_op jit(solution)/shard_map/dot_general | solution.py:489
  4.8 0.0 copy-done.3
  4.8 1.9 convolution_add_fusion.part_ref
  6.6 46.6 %shard_map.82.sum_ref = bf16[896,512]{1,0:T(8,128)(2,1)} custom-call(f32[896,512]{1,0:T(8,128)} %convolution_add_fusion.part_ref, s32[32]{0:T(128)} %cluster_ref.1), custom_call_target="tpu_custom_call" | custom-call | flops 10000000000 | bytes 3670016 | tf_op jit(solution)/shard_map/pallas_call | solution.py:168
  53.2 2.6 %fusion.7 = f32[512,256]{1,0:T(8,128)} fusion(bf16[896,512]{1,0:T(8,128)(2,1)} %shard_map.82.sum_ref, s32[]{:T(128)S(6)} %select_n.16), kind=kOutput, calls=%fused_computation.14 | convolution fusion | flops 234881024 | bytes 1900548 | tf_op jit(solution)/shard_map/dot_general | solution.py:480
  55.8 0.0 copy-start.4
  55.8 0.0 copy-start.5
  55.8 127.2 %shard_map.83 = bf16[32,24,896]{2,1,0:T(8,128)(2,1)} custom-call(f32[8,64,256]{2,1,0:T(8,128)} %bitcast.44, bf16[512,896]{1,0:T(8,128)(2,1)} %bitcast.43, bf16[32,24,896]{2,1,0:T(8,128)(2,1)} %bitcast.37, bf16[896,512]{1,0:T(8,128)(2,1)} %shard_map.82.sum_ref, bf16[896,512]{1,0:T(8,128)(2,1)} %bitcast.39, bf16[896,512]{1,0:T(8,128)(2,1)} %bitcast.38), custom_call_target="tpu_custom_call" | custom-call | flops 99999997952 | bytes 2097152 | tf_op jit(solution)/shard_map/pallas_call | solution.py:450
  183.0 0.0 copy-start.1
  183.0 0.0 copy-done.4
  183.0 0.0 copy-done.5
  183.1 1.8 convolution_bitcast_fusion.1
  184.9 0.0 copy-done.1
  184.9 1.0 fusion.1
  (2 shorter events, 0.1 us)
Async XLA Ops:
  0.0 1.2 copy-start
  0.0 2.9 %copy-start.2 = (bf16[1,2,512,512]{3,2,1,0:T(8,128)(2,1)S(1)}, bf16[1,2,512,512]{3,2,1,0:T(8,128)(2,1)}, u32[]{:S(2)}) copy-start(bf16[1,2,512,512]{3,2,1,0:T(8,128)(2,1)} %param.12) | copy-start | bytes 3145732
  2.9 1.9 %copy-start.3 = (bf16[1,896,512]{2,1,0:T(8,128)(2,1)S(1)}, bf16[1,896,512]{2,1,0:T(8,128)(2,1)}, u32[]{:S(2)}) copy-start(bf16[1,896,512]{2,1,0:T(8,128)(2,1)} %param.10) | copy-start | bytes 2752516
  55.8 127.2 %copy-start.4 = (s32[64,8]{0,1:T(8,128)S(1)}, s32[64,8]{0,1:T(8,128)}, u32[]{:S(2)}) copy-start(s32[64,8]{0,1:T(8,128)} %param.14) | copy-start | bytes 6148
  55.8 127.2 %copy-start.5 = (f32[64,8]{0,1:T(8,128)S(1)}, f32[64,8]{0,1:T(8,128)}, u32[]{:S(2)}) copy-start(f32[64,8]{0,1:T(8,128)} %param.15) | copy-start | bytes 6148
  183.0 1.9 %copy-start.1 = (bf16[32,24,896]{2,1,0:T(8,128)(2,1)S(1)}, bf16[32,24,896]{2,1,0:T(8,128)(2,1)}, u32[]{:S(2)}) copy-start(bf16[32,24,896]{2,1,0:T(8,128)(2,1)} %shard_map.83) | copy-start | bytes 4128772

commit v7 on v6

--- a/solution.py
+++ b/solution.py
@@ -348,7 +348,6 @@
         landing(lax.rem(expert + step, experts)).wait_recv()
         return carry
 
-    lax.fori_loop(1, experts, settle, 0)
     group = raw_part.shape[1] // capacity
 
     def project(index, carry):
@@ -357,10 +356,23 @@
             rows.astype(jnp.bfloat16), sum_ref[...], preferred_element_type=jnp.float32).astype(jnp.bfloat16)
         return carry
 
-    lax.fori_loop(0, experts // group, project, 0)
-    for side in range(2):
-        first(1, side).start()
-    eliminate(work, inv_ref, serve)
+    def service(kind, turn):
+        if kind == 0:
+            serve(0, turn)
+        else:
+            @pl.when(turn == 1)
+            def _():
+                lax.fori_loop(1, experts, settle, 0)
+                lax.fori_loop(0, experts // group, project, 0)
+                for side in range(2):
+                    first(1, side).start()
+
+            @pl.when(turn >= 2)
+            def _():
+                serve(1, turn - 2)
+
+    eliminate(work, inv_ref, service)
+    serve(1, count - 2)
     high = work[...].astype(jnp.bfloat16)
     high_ref[...] = high
     low_ref[...] = (work[...] - high.astype(jnp.float32)).astype(jnp.bfloat16)
@@ -377,6 +389,8 @@
         block = jnp.concatenate([coeff_all[side, piece, pick] for piece in range(count)], axis=0)
         final[index] = (jnp.dot(high, block, preferred_element_type=jnp.float32)
                         + jnp.dot(low, block, preferred_element_type=jnp.float32)).astype(jnp.bfloat16)
+
+    serve(1, count - 1)
 
     def give(target):
         return remote(answers.at[target], back_ref.at[expert], ans_send.at[target], ans_recv.at[expert], {"expert": target})

time: 187 us -> 183 us (0.979)
  Pallas kernels: 174 us -> 170 us
    pallas_call x1, Pallas kernels: 127 us -> 123 us  [expert_answers(): pl.pallas_call(whole_kernel, out_shape=jax.ShapeDtypeStruct(outgoing.shap...]
where the time goes in v7:
time: 183 us; the launch traced here: 182 us
  Pallas kernels  170 us (93%)
  matrix products  10.9 us (6%)
    pallas_call x1, Pallas kernels, expert_answers(): pl.pallas_call(whole_kernel, out_shape=jax.ShapeDtypeStruct(outgoing.shap...  123 us
    pallas_call x1, Pallas kernels, cluster_sum(): pl.pallas_call(cluster_kernel, out_shape=jax.ShapeDtypeStruct((rows, rank...  46.6 us
    dot_general x3, matrix products, transposed_dot(): lax.dot_general(left, right, (((0,), (0,)), ((), ())), preferred_element_...  5.43 us

profile of v7, /device:TPU:6, one launch (start us, length us, event | category | flops | bytes accessed | tf_op | source)
XLA Modules:
  0.0 181.7 jit_solution(5729292594607244057)
XLA Ops:
  0.0 0.0 copy-start
  0.0 0.0 copy-start.2
  0.0 0.8 fusion.21
  0.8 0.1 convolution_convert_fusion.1
  1.0 0.1 eq.48
  1.1 0.2 fusion.11
  1.2 0.0 copy-done
  1.3 1.6 convolution_convert_fusion
  2.9 0.0 copy-done.2
  2.9 0.0 copy-start.3
  2.9 1.9 %fusion.3 = f32[896,512]{1,0:T(8,128)S(1)} fusion(bf16[1,2,512,512]{3,2,1,0:T(8,128)(2,1)S(1)} %copy-done.2, bf16[1,896,512]{2,1,0:T(8,128)(2,1)} %param.9), kind=kOutput, calls=%fused_computation.8 | convolution fusion | flops 469762048 | bytes 3276800 | tf_op jit(solution)/shard_map/dot_general | solution.py:503
  4.8 0.0 copy-done.3
  4.8 1.9 %convolution_add_fusion.part_ref = f32[896,512]{1,0:T(8,128)} fusion(f32[896,512]{1,0:T(8,128)S(1)} %fusion.3, bf16[1,2,512,512]{3,2,1,0:T(8,128)(2,1)S(1)} %copy-done.2, bf16[1,896,512]{2,1,0:T(8,128)(2,1)S(1)} %copy-done.3), kind=kOutput, calls=%fused_computation.1 | convolution fusion | flops 470220800 | bytes 5111808 | tf_op jit(solution)/shard_map/dot_general | solution.py:503
  6.6 46.6 %shard_map.82.sum_ref = bf16[896,512]{1,0:T(8,128)(2,1)} custom-call(f32[896,512]{1,0:T(8,128)} %convolution_add_fusion.part_ref, s32[32]{0:T(128)} %cluster_ref.1), custom_call_target="tpu_custom_call" | custom-call | flops 10000000000 | bytes 3670016 | tf_op jit(solution)/shard_map/pallas_call | solution.py:168
  53.2 2.6 %fusion.7 = f32[512,256]{1,0:T(8,128)} fusion(bf16[896,512]{1,0:T(8,128)(2,1)} %shard_map.82.sum_ref, s32[]{:T(128)S(6)} %select_n.16), kind=kOutput, calls=%fused_computation.14 | convolution fusion | flops 234881024 | bytes 1900548 | tf_op jit(solution)/shard_map/dot_general | solution.py:494
  55.8 0.0 copy-start.4
  55.8 0.0 copy-start.5
  55.8 123.0 %shard_map.83 = bf16[32,24,896]{2,1,0:T(8,128)(2,1)} custom-call(f32[8,64,256]{2,1,0:T(8,128)} %bitcast.44, bf16[512,896]{1,0:T(8,128)(2,1)} %bitcast.43, bf16[32,24,896]{2,1,0:T(8,128)(2,1)} %bitcast.37, bf16[896,512]{1,0:T(8,128)(2,1)} %shard_map.82.sum_ref, bf16[896,512]{1,0:T(8,128)(2,1)} %bitcast.39, bf16[896,512]{1,0:T(8,128)(2,1)} %bitcast.38), custom_call_target="tpu_custom_call" | custom-call | flops 99999997952 | bytes 2097152 | tf_op jit(solution)/shard_map/pallas_call | solution.py:464
  178.8 0.0 copy-start.1
  178.8 0.0 copy-done.4
  178.8 0.0 copy-done.5
  178.9 1.8 convolution_bitcast_fusion.1
  180.7 0.0 copy-done.1
  180.7 1.0 fusion.1
  (2 shorter events, 0.1 us)
Async XLA Ops:
  0.0 1.2 copy-start
  0.0 2.9 %copy-start.2 = (bf16[1,2,512,512]{3,2,1,0:T(8,128)(2,1)S(1)}, bf16[1,2,512,512]{3,2,1,0:T(8,128)(2,1)}, u32[]{:S(2)}) copy-start(bf16[1,2,512,512]{3,2,1,0:T(8,128)(2,1)} %param.12) | copy-start | bytes 3145732
  2.9 1.9 %copy-start.3 = (bf16[1,896,512]{2,1,0:T(8,128)(2,1)S(1)}, bf16[1,896,512]{2,1,0:T(8,128)(2,1)}, u32[]{:S(2)}) copy-start(bf16[1,896,512]{2,1,0:T(8,128)(2,1)} %param.10) | copy-start | bytes 2752516
  55.8 123.0 %copy-start.4 = (s32[64,8]{0,1:T(8,128)S(1)}, s32[64,8]{0,1:T(8,128)}, u32[]{:S(2)}) copy-start(s32[64,8]{0,1:T(8,128)} %param.14) | copy-start | bytes 6148
  55.8 123.0 %copy-start.5 = (f32[64,8]{0,1:T(8,128)S(1)}, f32[64,8]{0,1:T(8,128)}, u32[]{:S(2)}) copy-start(f32[64,8]{0,1:T(8,128)} %param.15) | copy-start | bytes 6148
  178.8 1.9 %copy-start.1 = (bf16[32,24,896]{2,1,0:T(8,128)(2,1)S(1)}, bf16[32,24,896]{2,1,0:T(8,128)(2,1)}, u32[]{:S(2)}) copy-start(bf16[32,24,896]{2,1,0:T(8,128)(2,1)} %shard_map.83) | copy-start | bytes 4128772
